TPU v7x, 32 devices: a whole 2x2x4 slice. The times are simulated.
32 devices in a mesh: groups: 2 (over x), dev: 16 (over z, y, core).
Axes of the slice: x: 2, y: 2, z: 4, core: 2. Of those that a mesh axis runs over, the one named last changes fastest.
Arguments:
- queries: bfloat16 [2, 32, 128, 1024], P(None, ('groups', 'dev')), parts along dimension 1, may hold values from -180 to 180
- keys_values: bfloat16 [2, 32, 2, 1664, 128], P(None, ('groups', 'dev')), parts along dimension 1, may hold values from -6 to 6
- residual: bfloat16 [2, 2048, 2048], P(None, ('groups', 'dev')), parts along dimension 1, may hold values from -6 to 6
- norm_gain: float32 [2048], replicated, may hold values from 0.1 to 1.9
- gate_up: bfloat16 [16, 2048, 1536], P('dev'), may hold values from -0.125 to 0.125
- down_proj: bfloat16 [16, 768, 2048], P('dev'), may hold values from -0.21875 to 0.21875
- expert_ids: int32 [2, 2048, 8], P(None, ('groups', 'dev')), parts along dimension 1, may hold values from 0 to 15, all different within a row; in each aligned block of 64 rows (0 to 63, 64 to 127, ..., all dimensions but the last counted through in order) at most 40 rows name the same one
- expert_gates: int32 [2, 2048, 8], P(None, ('groups', 'dev')), parts along dimension 1, may hold values from 1 to 1023
Outputs:
- layer_out: bfloat16 [2, 2048, 2048], P(None, ('groups', 'dev')), parts along dimension 1
There are 2 independent parts, one for each index of `groups`. A program takes and returns all parts, laid end to end along the dimension named above; an argument that names none is the same for every part. Nothing has to cross between parts.
Inputs may be any that keep to these rules, and one draw needn't show every extreme that they name: `expert_ids`: in each micro-batch and each aligned block of 64 rows (the tokens of one device), no expert is named by more than 40 rows, a bound that some block reaches; the 8 experts of a row differ.
All inputs are finite; a program needn't handle non-finite values.
Results may differ from a plain program's by a relative error of at most 0.0039.
Values may be sent and summed in bfloat16 or wider, within the bound.
A program may use at most 128 MiB of HBM per device.

v0:
```python
import math

import jax
import jax.numpy as jnp
from jax import lax
from jax.sharding import PartitionSpec as P


def attend(query_rows, cached_pairs):
    batches, length, feat_width = query_rows.shape
    context = cached_pairs.shape[2]
    head_size = cached_pairs.shape[3]
    groups = feat_width // head_size
    head_rows = query_rows.reshape(batches, length, groups, head_size)
    scores = jnp.einsum(
        "mqgd,mkd->mgqk", head_rows, cached_pairs[:, 0], preferred_element_type=jnp.float32
    ) / math.sqrt(head_size)
    query_pos = context - length + lax.broadcasted_iota(jnp.int32, (length, context), 0)
    key_pos = lax.broadcasted_iota(jnp.int32, (length, context), 1)
    allowed = key_pos <= query_pos
    scores = jnp.where(allowed, scores, -1e30)
    highest = jnp.max(scores, axis=-1, keepdims=True)
    scaled_exp = jnp.where(allowed, jnp.exp(scores - highest), 0.0)
    totals = jnp.sum(scaled_exp, axis=-1, keepdims=True)
    weights = (scaled_exp / totals).astype(jnp.bfloat16)
    blended = jnp.einsum(
        "mgqk,mkd->mqgd", weights, cached_pairs[:, 1], preferred_element_type=jnp.float32
    )
    return blended.astype(jnp.bfloat16).reshape(batches, length, feat_width)


def to_owners(exchanged, kv_heads):
    batches, sources, positions, feat_width = exchanged.shape
    grouped = exchanged.reshape(batches, sources // kv_heads, kv_heads, positions, feat_width)
    grouped = jnp.transpose(grouped, (0, 1, 3, 2, 4))
    return grouped.reshape(batches, sources // kv_heads * positions, kv_heads * feat_width)


def prepare(attn_rows, residual, norm_gain, expert_ids, expert_gates, experts, capacity):
    stream = residual.astype(jnp.float32) + attn_rows.astype(jnp.float32)
    meansq = jnp.mean(stream * stream, axis=-1, keepdims=True)
    normed = (stream * lax.rsqrt(meansq + 1e-06) * norm_gain).astype(jnp.bfloat16)
    batches, rows_count, top_count = expert_ids.shape
    flat_ids = expert_ids.reshape(batches, rows_count * top_count)
    one_hot = (flat_ids[:, :, None] == jnp.arange(experts, dtype=jnp.int32)).astype(jnp.int32)
    ranking = jnp.sum((jnp.cumsum(one_hot, axis=1) - one_hot) * one_hot, axis=-1)
    target = flat_ids * capacity + ranking
    buffer_rows = jnp.arange(experts * capacity, dtype=jnp.int32)
    chosen = target.reshape(batches, 1, rows_count, top_count) == buffer_rows[None, :, None, None]
    selector = jnp.any(chosen, axis=-1).astype(jnp.bfloat16)
    outgoing = jnp.einsum(
        "mrt,mtd->mrd", selector, normed, preferred_element_type=jnp.float32
    ).astype(jnp.bfloat16)
    shares = expert_gates.astype(jnp.float32)
    shares = shares / jnp.sum(shares, axis=-1, keepdims=True)
    return (stream, outgoing, target, shares)


def run_experts(arrived, gate_up, down_proj):
    batches, sources, slot_count, model_width = arrived.shape
    local_count = gate_up.shape[0]
    hidden_width = down_proj.shape[1]
    per_expert = arrived.reshape(
        batches, sources, local_count, slot_count // local_count, model_width
    )
    rows_in = per_expert[:, :, 0].reshape(-1, model_width)
    projected = jnp.dot(rows_in, gate_up[0], preferred_element_type=jnp.float32)
    hidden = (jax.nn.silu(projected[:, :hidden_width]) * projected[:, hidden_width:]).astype(
        jnp.bfloat16
    )
    output = jnp.dot(hidden, down_proj[0], preferred_element_type=jnp.float32).astype(jnp.bfloat16)
    results = output.reshape(batches, sources, 1, slot_count // local_count, model_width)
    finished = results.reshape(batches, sources, slot_count, model_width)
    return lax.all_to_all(finished, "dev", split_axis=1, concat_axis=1, tiled=True)


def combine(came_back, target, shares, stream):
    batches, sources, slot_count, model_width = came_back.shape
    flat_back = came_back.reshape(batches, sources * slot_count, model_width)
    picked = jnp.take_along_axis(flat_back, target[:, :, None], axis=1)
    picked = picked.reshape(batches, shares.shape[1], shares.shape[2], model_width)
    summed = jnp.sum(shares[..., None] * picked.astype(jnp.float32), axis=2)
    return (stream + summed).astype(jnp.bfloat16)


def body(queries, keys_values, residual, norm_gain, gate_up, down_proj, expert_ids, expert_gates):
    devices = lax.axis_size("dev")
    model_width = residual.shape[2]
    kv_heads = model_width // queries.shape[3]
    experts = devices * gate_up.shape[0]
    capacity = 5 * residual.shape[1] * expert_ids.shape[2] // (4 * experts)
    own_query = queries[:, 0]
    own_pairs = keys_values[:, 0]
    batches, length, feat_width = own_query.shape
    positions = length // devices
    pieces = []
    for batch_index in range(batches):
        window = slice(batch_index, batch_index + 1)
        blended_heads = attend(own_query[window], own_pairs[window])
        outgoing_rows = blended_heads.reshape(1, devices, positions, feat_width)
        arrived_rows = lax.all_to_all(outgoing_rows, "dev", split_axis=1, concat_axis=1, tiled=True)
        attn_rows = to_owners(arrived_rows, kv_heads)
        stream, dispatched, target, shares = prepare(
            attn_rows,
            residual[window],
            norm_gain,
            expert_ids[window],
            expert_gates[window],
            experts,
            capacity,
        )
        shaped = dispatched.reshape(1, devices, -1, model_width)
        came_back = run_experts(
            lax.all_to_all(shaped, "dev", split_axis=1, concat_axis=1, tiled=True),
            gate_up,
            down_proj,
        )
        pieces.append(combine(came_back, target, shares, stream))
    return jnp.concatenate(pieces, axis=0)


def solution(mesh):
    in_specs = (
        P(None, ("groups", "dev"), None, None),
        P(None, ("groups", "dev"), None, None, None),
        P(None, ("groups", "dev"), None),
        P(),
        P("dev", None, None),
        P("dev", None, None),
        P(None, ("groups", "dev"), None),
        P(None, ("groups", "dev"), None),
    )
    out_specs = P(None, ("groups", "dev"), None)
    return jax.shard_map(body, mesh=mesh, in_specs=in_specs, out_specs=out_specs, check_vma=False)
```

profile of v0, /device:TPU:13, one launch (start us, length us, event | category | flops | bytes accessed | tf_op | source)
XLA Modules:
  0.0 324.9 jit_solution(10127047366721078004)
XLA Ops:
  0.0 0.1 iota_compare_fusion.2
  0.2 2.9 slice_bitcast_fusion
  3.0 0.8 fusion.58
  3.9 1.8 copy.85
  5.6 1.8 copy.87
  7.5 2.3 fusion.4
  9.7 2.8 fusion.6
  12.6 1.6 fusion.7
  14.2 2.6 fusion.26
  16.8 0.9 copy.72
  17.6 1.8 reshape_reshape.14
  19.4 6.5 %all-to-all-start.3 = ((bf16[1,16,8,1024]{3,2,0,1:T(8,128)(2,1)}), bf16[1,16,8,1024]{3,2,0,1:T(8,128)(2,1)}, u32[]{:S(2)}, u32[]{:S(2)}) async-start(bf16[1,16,8,1024]{3,2,0,1:T(8,128)(2,1)} %bitcast.227), calls=%async_computation.3 | async-start | bytes 524288 | tf_op jit(solution)/shard_map/all_to_all | solution.py:101
  25.9 5.5 %fusion.29 = bf16[1,128,8,128]{3,1,2,0:T(8,128)(2,1)S(1)} fusion(f32[8,128]{1,0:T(8,128)S(1)} %get-tuple-element.8, f32[8,128]{1,0:T(8,128)S(1)} %get-tuple-element.26, f32[1664,128,8]{1,0,2:T(8,128)} %copy-done.1, pred[128,1664]{0,1:T(8,128)(4,1)S(1)} %iota_compare_fusion.2, bf16[1,2,1664,128]{3,2,1,0:T(8,128)(2,1)} %get-tuple-element.17), kind=kOutput, calls=%fused_computation.43 | convolution fusion | flops 446562304 | bytes 7725056 | tf_op jit(solution)/shard_map/mgqk,mkd->mqgd/dot_general | solution.py:26
  31.4 0.0 copy-start.10
  31.5 0.2 copy.60
  31.6 0.8 reshape_reshape.12
  32.5 0.1 copy.88
  32.5 0.1 eq.103
  32.7 1.2 reduce-window.16
  33.8 0.2 slice_reduce_fusion
  34.1 6.0 %all-to-all-start = ((bf16[1,16,8,1024]{3,2,0,1:T(8,128)(2,1)}), bf16[1,16,8,1024]{3,2,0,1:T(8,128)(2,1)S(1)}, u32[]{:S(2)}, u32[]{:S(2)}) async-start(bf16[1,16,8,1024]{3,2,0,1:T(8,128)(2,1)} %bitcast.226), calls=%async_computation | async-start | bytes 524288 | tf_op jit(solution)/shard_map/all_to_all | solution.py:101
  40.1 0.1 copy.78
  40.2 0.1 broadcast.280
  40.3 0.1 fusion.49
  40.4 0.1 reduce_sum.113
  40.5 0.5 fusion.19
  41.0 1.8 convert.10
  42.8 5.3 %all-to-all-done = bf16[1,16,8,1024]{3,2,0,1:T(8,128)(2,1)S(1)} async-done(((bf16[1,16,8,1024]{3,2,0,1:T(8,128)(2,1)}), bf16[1,16,8,1024]{3,2,0,1:T(8,128)(2,1)S(1)}, u32[]{:S(2)}, u32[]{:S(2)}) %all-to-all-start) | async-done | bytes 262176 | tf_op jit(solution)/shard_map/all_to_all | solution.py:101
  48.1 0.8 copy-done.4
  49.0 1.4 multiply_reduce_fusion.1
  50.4 3.6 %convolution_convert_fusion.2 = bf16[640,2048]{1,0:T(8,128)(2,1)} fusion(pred[640,64]{0,1:T(8,128)(4,1)S(1)} %fusion.19, f32[64]{0:T(128)S(1)} %get-tuple-element.29, f32[2048]{0:T(1024)S(1)} %copy-done.10, f32[1,64,2048]{2,1,0:T(8,128)} %bitcast.217, bf16[2,64,2048]{2,1,0:T(8,128)(2,1)} %param.12), kind=kOutput, calls=%fused_computation.26 | convolution fusion | flops 169738240 | bytes 3457280 | tf_op jit(solution)/shard_map/mrt,mtd->mrd/dot_general | solution.py:51
  54.0 6.4 %all-to-all-start.4 = ((bf16[1,16,40,2048]{3,2,0,1:T(8,128)(2,1)}), bf16[1,16,40,2048]{3,2,0,1:T(8,128)(2,1)}, u32[]{:S(2)}, u32[]{:S(2)}) async-start(bf16[1,16,40,2048]{3,2,0,1:T(8,128)(2,1)} %bitcast.214), calls=%async_computation.4 | async-start | bytes 5242880 | tf_op jit(solution)/shard_map/all_to_all | solution.py:114
  60.3 0.1 copy.86
  60.4 0.1 eq.96
  60.6 1.2 reduce-window.14
  61.7 0.2 slice_reduce_fusion.1
  62.0 0.1 copy.66
  62.1 0.1 broadcast.276
  62.2 0.1 fusion.48
  62.3 0.1 reduce_sum.105
  62.4 0.5 fusion.18
  62.8 3.5 %convolution_convert_fusion.3 = bf16[640,2048]{1,0:T(8,128)(2,1)} fusion(pred[640,64]{0,1:T(8,128)(4,1)S(1)} %fusion.18, f32[2048]{0:T(1024)S(1)} %copy-done.10, f32[64]{0:T(128)S(1)} %get-tuple-element.30, f32[1,64,2048]{2,1,0:T(8,128)} %bitcast.220, bf16[2,64,2048]{2,1,0:T(8,128)(2,1)} %param.12), kind=kOutput, calls=%fused_computation.27 | convolution fusion | flops 169738240 | bytes 3457280 | tf_op jit(solution)/shard_map/mrt,mtd->mrd/dot_general | solution.py:51
  66.4 52.8 %all-to-all-done.4 = bf16[1,16,40,2048]{3,2,0,1:T(8,128)(2,1)} async-done(((bf16[1,16,40,2048]{3,2,0,1:T(8,128)(2,1)}), bf16[1,16,40,2048]{3,2,0,1:T(8,128)(2,1)}, u32[]{:S(2)}, u32[]{:S(2)}) %all-to-all-start.4) | async-done | bytes 2621472 | tf_op jit(solution)/shard_map/all_to_all | solution.py:114
  119.1 4.8 %all-to-all-start.1 = ((bf16[1,16,40,2048]{3,2,0,1:T(8,128)(2,1)}), bf16[1,16,40,2048]{3,2,0,1:T(8,128)(2,1)}, u32[]{:S(2)}, u32[]{:S(2)}) async-start(bf16[1,16,40,2048]{3,2,0,1:T(8,128)(2,1)} %bitcast.215), calls=%async_computation.1 | async-start | bytes 5242880 | tf_op jit(solution)/shard_map/all_to_all | solution.py:114
  123.9 7.1 %fusion = f32[640,1536]{1,0:T(8,128)S(1)} fusion(bf16[640,2048]{1,0:T(8,128)(2,1)} %bitcast.67, bf16[1,2048,1536]{2,1,0:T(8,128)(2,1)} %param.14), kind=kOutput, calls=%fused_computation.8 | convolution fusion | flops 4026531840 | bytes 12845056 | tf_op jit(solution)/shard_map/dot_general | solution.py:67
  131.0 3.8 %convolution_convert_fusion = bf16[640,2048]{1,0:T(8,128)(2,1)} fusion(bf16[1,768,2048]{2,1,0:T(8,128)(2,1)S(1)} %copy-done, f32[640,1536]{1,0:T(8,128)S(1)} %fusion), kind=kOutput, calls=%fused_computation.24 | convolution fusion | flops 2017525760 | bytes 9699328 | tf_op jit(solution)/shard_map/dot_general | solution.py:71
  134.8 47.8 %all-to-all-done.1 = bf16[1,16,40,2048]{3,2,0,1:T(8,128)(2,1)} async-done(((bf16[1,16,40,2048]{3,2,0,1:T(8,128)(2,1)}), bf16[1,16,40,2048]{3,2,0,1:T(8,128)(2,1)}, u32[]{:S(2)}, u32[]{:S(2)}) %all-to-all-start.1) | async-done | bytes 2621472 | tf_op jit(solution)/shard_map/all_to_all | solution.py:114
  182.6 4.8 %all-to-all-start.5 = ((bf16[1,16,40,2048]{3,2,0,1:T(8,128)(2,1)}), bf16[1,16,40,2048]{3,2,0,1:T(8,128)(2,1)}, u32[]{:S(2)}, u32[]{:S(2)}) async-start(bf16[1,16,40,2048]{3,2,0,1:T(8,128)(2,1)} %bitcast.223), calls=%async_computation.5 | async-start | bytes 5242880 | tf_op jit(solution)/shard_map/all_to_all | solution.py:74
  187.4 7.1 %fusion.2 = f32[640,1536]{1,0:T(8,128)S(1)} fusion(bf16[640,2048]{1,0:T(8,128)(2,1)} %bitcast.28, bf16[1,2048,1536]{2,1,0:T(8,128)(2,1)} %param.14), kind=kOutput, calls=%fused_computation.10 | convolution fusion | flops 4026531840 | bytes 12845056 | tf_op jit(solution)/shard_map/dot_general | solution.py:67
  194.6 3.7 %convolution_convert_fusion.1 = bf16[640,2048]{1,0:T(8,128)(2,1)} fusion(bf16[1,768,2048]{2,1,0:T(8,128)(2,1)S(1)} %copy-done, f32[640,1536]{1,0:T(8,128)S(1)} %fusion.2), kind=kOutput, calls=%fused_computation.25 | convolution fusion | flops 2017525760 | bytes 9699328 | tf_op jit(solution)/shard_map/dot_general | solution.py:71
  198.3 47.9 %all-to-all-done.5 = bf16[1,16,40,2048]{3,2,0,1:T(8,128)(2,1)} async-done(((bf16[1,16,40,2048]{3,2,0,1:T(8,128)(2,1)}), bf16[1,16,40,2048]{3,2,0,1:T(8,128)(2,1)}, u32[]{:S(2)}, u32[]{:S(2)}) %all-to-all-start.5) | async-done | bytes 2621472 | tf_op jit(solution)/shard_map/all_to_all | solution.py:74
  246.2 4.8 %all-to-all-start.2 = ((bf16[1,16,40,2048]{3,2,0,1:T(8,128)(2,1)}), bf16[1,16,40,2048]{3,2,0,1:T(8,128)(2,1)}, u32[]{:S(2)}, u32[]{:S(2)}) async-start(bf16[1,16,40,2048]{3,2,0,1:T(8,128)(2,1)} %bitcast.222), calls=%async_computation.2 | async-start | bytes 5242880 | tf_op jit(solution)/shard_map/all_to_all | solution.py:74
  251.0 0.1 mul.166
  251.1 0.1 copy.74
  251.2 0.1 mul.153
  251.3 0.1 copy.62
  251.5 7.4 %gather_fusion.1 = bf16[512,2048]{1,0:T(8,128)(2,1)} fusion(bf16[640,2048]{1,0:T(8,128)(2,1)} %bitcast.71, s32[1024]{0:T(1024)S(1)} %pad_clamp_fusion), kind=kCustom, calls=%fused_computation.1.clone | custom fusion | bytes 4196352 | tf_op jit(solution)/shard_map/jit(take_along_axis)/gather | solution.py:80
  258.8 50.9 %all-to-all-done.2 = bf16[1,16,40,2048]{3,2,0,1:T(8,128)(2,1)} async-done(((bf16[1,16,40,2048]{3,2,0,1:T(8,128)(2,1)}), bf16[1,16,40,2048]{3,2,0,1:T(8,128)(2,1)}, u32[]{:S(2)}, u32[]{:S(2)}) %all-to-all-start.2) | async-done | bytes 2621472 | tf_op jit(solution)/shard_map/all_to_all | solution.py:74
  309.7 7.4 %gather_fusion = bf16[512,2048]{1,0:T(8,128)(2,1)} fusion(bf16[640,2048]{1,0:T(8,128)(2,1)} %bitcast.34, s32[1024]{0:T(1024)S(1)} %pad_clamp_fusion.1), kind=kCustom, calls=%fused_computation.clone | custom fusion | bytes 4196352 | tf_op jit(solution)/shard_map/jit(take_along_axis)/gather | solution.py:80
  317.1 4.2 %fusion.8 = f32[64,2048]{1,0:T(8,128)S(1)} fusion(bf16[512,2048]{1,0:T(8,128)(2,1)} %gather_fusion.1, f32[64,8]{1,0:T(8,128)S(1)} %copy.74, pred[512]{0:T(512)(128)(4,1)S(1)} %get-tuple-element.14), kind=kLoop, calls=%fused_computation.17 | loop fusion | flops 4063232 | bytes 2624000 | tf_op jit(solution)/shard_map/reduce_sum | solution.py:82
  321.3 2.5 fusion.9
  323.9 0.2 fusion.37
  324.1 0.0 copy-start.14
  324.1 0.8 copy-done.14
  (52 shorter events, 0.4 us)
Async XLA Ops:
  0.0 131.0 %copy-start = (bf16[1,768,2048]{2,1,0:T(8,128)(2,1)S(1)}, bf16[1,768,2048]{2,1,0:T(8,128)(2,1)}, u32[]{:S(2)}) copy-start(bf16[1,768,2048]{2,1,0:T(8,128)(2,1)} %param.15) | copy-start | bytes 9437188
  0.0 3.0 copy-start.8
  7.4 2.3 copy-start.7
  7.5 2.3 copy-start.9
  9.7 2.8 copy-start.1
  19.4 14.7 %all-to-all-start.3 = ((bf16[1,16,8,1024]{3,2,0,1:T(8,128)(2,1)}), bf16[1,16,8,1024]{3,2,0,1:T(8,128)(2,1)}, u32[]{:S(2)}, u32[]{:S(2)}) async-start(bf16[1,16,8,1024]{3,2,0,1:T(8,128)(2,1)} %bitcast.227), calls=%async_computation.3 | async-start | bytes 524288 | tf_op jit(solution)/shard_map/all_to_all | solution.py:101
  25.9 6.5 %copy-start.12 = (s32[2,64,8]{1,2,0:T(8,128)S(1)}, s32[2,64,8]{1,2,0:T(8,128)}, u32[]{:S(2)}) copy-start(s32[2,64,8]{1,2,0:T(8,128)} %param.16) | copy-start | bytes 12292
  31.4 19.0 %copy-start.10 = (f32[2048]{0:T(1024)S(1)}, f32[2048]{0:T(1024)}, u32[]{:S(2)}) copy-start(f32[2048]{0:T(1024)} %param.13) | copy-start | bytes 24580
  34.1 14.0 %all-to-all-start = ((bf16[1,16,8,1024]{3,2,0,1:T(8,128)(2,1)}), bf16[1,16,8,1024]{3,2,0,1:T(8,128)(2,1)S(1)}, u32[]{:S(2)}, u32[]{:S(2)}) async-start(bf16[1,16,8,1024]{3,2,0,1:T(8,128)(2,1)} %bitcast.226), calls=%async_computation | async-start | bytes 524288 | tf_op jit(solution)/shard_map/all_to_all | solution.py:101
  48.1 0.8 copy-start.4
  54.0 65.2 %all-to-all-start.4 = ((bf16[1,16,40,2048]{3,2,0,1:T(8,128)(2,1)}), bf16[1,16,40,2048]{3,2,0,1:T(8,128)(2,1)}, u32[]{:S(2)}, u32[]{:S(2)}) async-start(bf16[1,16,40,2048]{3,2,0,1:T(8,128)(2,1)} %bitcast.214), calls=%async_computation.4 | async-start | bytes 5242880 | tf_op jit(solution)/shard_map/all_to_all | solution.py:114
  119.1 63.5 %all-to-all-start.1 = ((bf16[1,16,40,2048]{3,2,0,1:T(8,128)(2,1)}), bf16[1,16,40,2048]{3,2,0,1:T(8,128)(2,1)}, u32[]{:S(2)}, u32[]{:S(2)}) async-start(bf16[1,16,40,2048]{3,2,0,1:T(8,128)(2,1)} %bitcast.215), calls=%async_computation.1 | async-start | bytes 5242880 | tf_op jit(solution)/shard_map/all_to_all | solution.py:114
  182.6 63.5 %all-to-all-start.5 = ((bf16[1,16,40,2048]{3,2,0,1:T(8,128)(2,1)}), bf16[1,16,40,2048]{3,2,0,1:T(8,128)(2,1)}, u32[]{:S(2)}, u32[]{:S(2)}) async-start(bf16[1,16,40,2048]{3,2,0,1:T(8,128)(2,1)} %bitcast.223), calls=%async_computation.5 | async-start | bytes 5242880 | tf_op jit(solution)/shard_map/all_to_all | solution.py:74
  198.3 52.8 %copy-start.11 = (s32[2,64,8]{1,2,0:T(8,128)S(1)}, s32[2,64,8]{1,2,0:T(8,128)}, u32[]{:S(2)}) copy-start(s32[2,64,8]{1,2,0:T(8,128)} %param.17) | copy-start | bytes 12292
  246.2 63.5 %all-to-all-start.2 = ((bf16[1,16,40,2048]{3,2,0,1:T(8,128)(2,1)}), bf16[1,16,40,2048]{3,2,0,1:T(8,128)(2,1)}, u32[]{:S(2)}, u32[]{:S(2)}) async-start(bf16[1,16,40,2048]{3,2,0,1:T(8,128)(2,1)} %bitcast.222), calls=%async_computation.2 | async-start | bytes 5242880 | tf_op jit(solution)/shard_map/all_to_all | solution.py:74
  317.1 4.2 %copy-start.2 = (bf16[512,2048]{1,0:T(8,128)(2,1)S(1)}, bf16[512,2048]{1,0:T(8,128)(2,1)}, u32[]{:S(2)}) copy-start(bf16[512,2048]{1,0:T(8,128)(2,1)} %gather_fusion) | copy-start | bytes 6291460
  317.1 6.8 %copy-start.3 = (f32[1,8,2,8,1024]{4,3,2,1,0:T(8,128)S(1)}, f32[1,8,2,8,1024]{4,3,2,1,0:T(8,128)}, u32[]{:S(2)}) copy-start(f32[1,8,2,8,1024]{4,3,2,1,0:T(8,128)} %convert.10) | copy-start | bytes 1572868
  317.1 6.8 %copy-start.5 = (f32[1,8,2,8,1024]{4,3,2,1,0:T(8,128)S(1)}, f32[1,8,2,8,1024]{4,3,2,1,0:T(8,128)}, u32[]{:S(2)}) copy-start(f32[1,8,2,8,1024]{4,3,2,1,0:T(8,128)} %copy-done.4) | copy-start | bytes 1572868
  317.1 6.8 %copy-start.6 = (bf16[2,64,2048]{2,1,0:T(8,128)(2,1)S(1)}, bf16[2,64,2048]{2,1,0:T(8,128)(2,1)}, u32[]{:S(2)}) copy-start(bf16[2,64,2048]{2,1,0:T(8,128)(2,1)} %param.12) | copy-start | bytes 1572868
  317.1 6.8 %copy-start.13 = (bf16[2,64,2048]{2,1,0:T(8,128)(2,1)S(1)}, bf16[2,64,2048]{2,1,0:T(8,128)(2,1)}, u32[]{:S(2)}) copy-start(bf16[2,64,2048]{2,1,0:T(8,128)(2,1)} %custom-call.4) | copy-start | bytes 1572868
  324.1 0.8 copy-start.14
where the time goes:
time: 326 us; the launch traced here: 325 us
  waiting for transfers between devices  205 us (63%)
  matrix products  42 us (13%)
  starting transfers between devices  33.2 us (10%)
  local copies, waits for them, and re-layouts  29 us (9%)
  other arithmetic  15.6 us (5%)
    all_to_all x2, waiting for transfers between devices, body(): lax.all_to_all(shaped, 'dev', split_axis=1, concat_axis=1, tiled=True)  101 us
    all_to_all x2, waiting for transfers between devices, run_experts(): lax.all_to_all(finished, 'dev', split_axis=1, concat_axis=1, tiled=True)  98.8 us
    gather x2, local copies, waits for them, and re-layouts, combine(): picked = jnp.take_along_axis(flat_back, target[:, :, None], axis=1)  14.7 us
    dot_general x2, matrix products, run_experts(): projected = jnp.dot(rows_in, gate_up[0], preferred_element_type=jnp.float32)  14.3 us
    all_to_all x2, starting transfers between devices, body(): lax.all_to_all(outgoing_rows, 'dev', split_axis=1, concat_axis=1, tiled=T...  12.5 us
    all_to_all x2, starting transfers between devices, body(): lax.all_to_all(shaped, 'dev', split_axis=1, concat_axis=1, tiled=True)  11.1 us
    all_to_all x2, starting transfers between devices, run_experts(): lax.all_to_all(finished, 'dev', split_axis=1, concat_axis=1, tiled=True)  9.56 us
    dot_general x2, matrix products, attend(): jnp.einsum('mgqk,mkd->mqgd', weights, cached_pairs[:, 1], preferred_eleme...  8.07 us
  transfers between devices with their start and end apart: 6, of which 5 were waited for; matrix products, arithmetic and copies ran while one was open for 14% of the time, Pallas kernels for 0%

commit v1 on v0

v1 whole, which is shorter than its diff:
```python
import math

import jax
import jax.numpy as jnp
from jax import lax
from jax.sharding import PartitionSpec as P


def attend(query_rows, cached_pairs):
    batches, length, feat_width = query_rows.shape
    context = cached_pairs.shape[2]
    head_size = cached_pairs.shape[3]
    groups = feat_width // head_size
    head_rows = query_rows.reshape(batches, length, groups, head_size)
    scores = jnp.einsum(
        "mqgd,mkd->mgqk", head_rows, cached_pairs[:, 0], preferred_element_type=jnp.float32
    ) / math.sqrt(head_size)
    query_pos = context - length + lax.broadcasted_iota(jnp.int32, (length, context), 0)
    key_pos = lax.broadcasted_iota(jnp.int32, (length, context), 1)
    allowed = key_pos <= query_pos
    scores = jnp.where(allowed, scores, -1e30)
    highest = jnp.max(scores, axis=-1, keepdims=True)
    scaled_exp = jnp.where(allowed, jnp.exp(scores - highest), 0.0)
    totals = jnp.sum(scaled_exp, axis=-1, keepdims=True)
    weights = (scaled_exp / totals).astype(jnp.bfloat16)
    blended = jnp.einsum(
        "mgqk,mkd->mqgd", weights, cached_pairs[:, 1], preferred_element_type=jnp.float32
    )
    return blended.astype(jnp.bfloat16).reshape(batches, length, feat_width)


def to_owners(exchanged, kv_heads):
    batches, sources, positions, feat_width = exchanged.shape
    grouped = exchanged.reshape(batches, sources // kv_heads, kv_heads, positions, feat_width)
    grouped = jnp.transpose(grouped, (0, 1, 3, 2, 4))
    return grouped.reshape(batches, sources // kv_heads * positions, kv_heads * feat_width)


def prepare(attn_rows, residual, norm_gain):
    stream = residual.astype(jnp.float32) + attn_rows.astype(jnp.float32)
    meansq = jnp.mean(stream * stream, axis=-1, keepdims=True)
    normed = (stream * lax.rsqrt(meansq + 1e-06) * norm_gain).astype(jnp.bfloat16)
    return stream, normed


def dense_shares(expert_ids, expert_gates, experts):
    shares = expert_gates.astype(jnp.float32)
    shares = shares / jnp.sum(shares, axis=-1, keepdims=True)
    named = expert_ids[..., None] == jnp.arange(experts, dtype=jnp.int32)
    return jnp.sum(jnp.where(named, shares[..., None], 0.0), axis=-2)


def run_expert(rows_in, gate_up, down_proj, weight):
    hidden_width = down_proj.shape[1]
    projected = jnp.dot(rows_in, gate_up[0], preferred_element_type=jnp.float32)
    hidden = (jax.nn.silu(projected[:, :hidden_width]) * projected[:, hidden_width:]).astype(
        jnp.bfloat16
    )
    output = jnp.dot(hidden, down_proj[0], preferred_element_type=jnp.float32)
    return (output * weight).astype(jnp.bfloat16)


def body(queries, keys_values, residual, norm_gain, gate_up, down_proj, expert_ids, expert_gates):
    devices = lax.axis_size("dev")
    me = lax.axis_index("dev")
    model_width = residual.shape[2]
    kv_heads = model_width // queries.shape[3]
    experts = devices * gate_up.shape[0]
    own_query = queries[:, 0]
    own_pairs = keys_values[:, 0]
    batches, length, feat_width = own_query.shape
    positions = length // devices
    weights = dense_shares(expert_ids, expert_gates, experts)
    weights = lax.all_gather(weights, "dev", axis=1, tiled=True)
    mine = jnp.sum(
        jnp.where(jnp.arange(experts, dtype=jnp.int32) == me, weights, 0.0), axis=-1, keepdims=True
    )
    pieces = []
    for batch_index in range(batches):
        window = slice(batch_index, batch_index + 1)
        blended_heads = attend(own_query[window], own_pairs[window])
        outgoing_rows = blended_heads.reshape(1, devices, positions, feat_width)
        arrived_rows = lax.all_to_all(outgoing_rows, "dev", split_axis=1, concat_axis=1, tiled=True)
        attn_rows = to_owners(arrived_rows, kv_heads)
        stream, normed = prepare(attn_rows[0], residual[batch_index], norm_gain)
        rows_in = lax.all_gather(normed, "dev", axis=0, tiled=True)
        partial = run_expert(rows_in, gate_up, down_proj, mine[batch_index])
        summed = lax.psum_scatter(partial, "dev", scatter_dimension=0, tiled=True)
        pieces.append((stream + summed.astype(jnp.float32)).astype(jnp.bfloat16))
    return jnp.stack(pieces, axis=0)


def solution(mesh):
    in_specs = (
        P(None, ("groups", "dev"), None, None),
        P(None, ("groups", "dev"), None, None, None),
        P(None, ("groups", "dev"), None),
        P(),
        P("dev", None, None),
        P("dev", None, None),
        P(None, ("groups", "dev"), None),
        P(None, ("groups", "dev"), None),
    )
    out_specs = P(None, ("groups", "dev"), None)
    return jax.shard_map(body, mesh=mesh, in_specs=in_specs, out_specs=out_specs, check_vma=False)
```

time: 326 us -> 325 us (level)
  the two profiles are of different devices: /device:TPU:13 before, /device:TPU:0 now
where the time goes in v1:
time: 325 us; the launch traced here: 324 us
  waiting for transfers between devices  205 us (63%)
  matrix products  43.3 us (13%)
  blocking collectives  24.2 us (7%)
  local copies, waits for them, and re-layouts  15.7 us (5%)
  between operations  13.4 us (4%)
  starting transfers between devices  11.3 us (3%)
  other arithmetic  11.2 us (3%)
    reduce_scatter x2, waiting for transfers between devices, body(): summed = lax.psum_scatter(partial, 'dev', scatter_dimension=0, tiled=True)  136 us
    all_gather x2, waiting for transfers between devices, body(): rows_in = lax.all_gather(normed, 'dev', axis=0, tiled=True)  57.3 us
    all_gather x1, blocking collectives, body(): weights = lax.all_gather(weights, 'dev', axis=1, tiled=True)  24.2 us
    dot_general x2, matrix products, run_expert(): projected = jnp.dot(rows_in, gate_up[0], preferred_element_type=jnp.float32)  20 us
    all_to_all x2, waiting for transfers between devices, body(): lax.all_to_all(outgoing_rows, 'dev', split_axis=1, concat_axis=1, tiled=T...  11.4 us
    all_to_all x2, starting transfers between devices, body(): lax.all_to_all(outgoing_rows, 'dev', split_axis=1, concat_axis=1, tiled=T...  11 us
    dot_general x2, matrix products, run_expert(): output = jnp.dot(hidden, down_proj[0], preferred_element_type=jnp.float32)  10.1 us
    dot_general x2, matrix products, attend(): jnp.einsum('mgqk,mkd->mqgd', weights, cached_pairs[:, 1], preferred_eleme...  8.07 us
  transfers between devices with their start and end apart: 6, of which 6 were waited for; matrix products, arithmetic and copies ran while one was open for 13% of the time, Pallas kernels for 0%

profile of v1, /device:TPU:0, one launch (start us, length us, event | category | flops | bytes accessed | tf_op | source)
XLA Modules:
  0.0 324.2 jit_solution(8662841246173468130)
XLA Ops:
  6.5 0.0 copy-start
  6.5 0.1 iota_compare_fusion
  6.7 2.9 slice_bitcast_fusion
  9.6 1.8 fusion.50
  11.4 1.8 copy.62
  13.2 1.8 copy.64
  15.0 0.0 copy-start.3
  15.0 0.0 copy-start.4
  15.0 2.3 fusion.4
  17.3 0.0 copy-start.1
  17.3 0.0 copy-done.3
  17.3 0.0 copy-done.4
  17.3 2.8 fusion.6
  20.1 0.0 copy-done.1
  20.1 1.6 fusion.7
  21.7 2.6 fusion.26
  24.3 0.9 copy.55
  25.2 1.8 reshape_reshape.7
  26.9 7.5 %all-to-all-start.1 = ((bf16[1,16,8,1024]{3,2,0,1:T(8,128)(2,1)}), bf16[1,16,8,1024]{3,2,0,1:T(8,128)(2,1)}, u32[]{:S(2)}, u32[]{:S(2)}) async-start(bf16[1,16,8,1024]{3,2,0,1:T(8,128)(2,1)} %bitcast.156), calls=%async_computation.2 | async-start | bytes 524288 | tf_op jit(solution)/shard_map/all_to_all | solution.py:83
  34.4 0.0 copy-start.5
  34.4 5.5 %fusion.29 = bf16[1,128,8,128]{3,1,2,0:T(8,128)(2,1)S(1)} fusion(f32[8,128]{1,0:T(8,128)S(1)} %get-tuple-element.7, f32[8,128]{1,0:T(8,128)S(1)} %get-tuple-element.19, f32[1664,128,8]{1,0,2:T(8,128)} %copy-done.1, pred[128,1664]{0,1:T(8,128)(4,1)S(1)} %iota_compare_fusion, bf16[1,2,1664,128]{3,2,1,0:T(8,128)(2,1)} %get-tuple-element.10), kind=kOutput, calls=%fused_computation.31 | convolution fusion | flops 446562304 | bytes 7725056 | tf_op jit(solution)/shard_map/mgqk,mkd->mqgd/dot_general | solution.py:26
  39.9 0.0 copy-start.7
  40.0 0.0 copy-start.6
  40.0 0.2 copy.48
  40.2 0.8 reshape_reshape.6
  41.0 3.5 %all-to-all-done.1 = bf16[1,16,8,1024]{3,2,0,1:T(8,128)(2,1)} async-done(((bf16[1,16,8,1024]{3,2,0,1:T(8,128)(2,1)}), bf16[1,16,8,1024]{3,2,0,1:T(8,128)(2,1)}, u32[]{:S(2)}, u32[]{:S(2)}) %all-to-all-start.1) | async-done | bytes 262176 | tf_op jit(solution)/shard_map/all_to_all | solution.py:83
  44.5 3.5 %all-to-all-start = ((bf16[1,16,8,1024]{3,2,0,1:T(8,128)(2,1)}), bf16[1,16,8,1024]{3,2,0,1:T(8,128)(2,1)S(1)}, u32[]{:S(2)}, u32[]{:S(2)}) async-start(bf16[1,16,8,1024]{3,2,0,1:T(8,128)(2,1)} %bitcast.157), calls=%async_computation | async-start | bytes 524288 | tf_op jit(solution)/shard_map/all_to_all | solution.py:83
  48.0 0.2 all-gather.5.cloned.1.call-start
  48.3 1.8 convert.11
  50.1 7.9 %all-to-all-done = bf16[1,16,8,1024]{3,2,0,1:T(8,128)(2,1)S(1)} async-done(((bf16[1,16,8,1024]{3,2,0,1:T(8,128)(2,1)}), bf16[1,16,8,1024]{3,2,0,1:T(8,128)(2,1)S(1)}, u32[]{:S(2)}, u32[]{:S(2)}) %all-to-all-start) | async-done | bytes 262176 | tf_op jit(solution)/shard_map/all_to_all | solution.py:83
  58.1 0.0 copy-start.2
  58.1 1.6 multiply_reduce_fusion.1
  59.7 0.0 copy-done.2
  59.7 0.0 copy-done.5
  59.7 2.2 multiply_convert_fusion.3
  61.9 0.0 all-gather.5.cloned.1.call-update
  61.9 0.0 all-gather.3.cloned.1.call-start
  62.0 0.7 all-gather.3.cloned.1.call-update
  62.7 0.0 reduce-scatter.5.cloned.1.call-start
  62.7 0.0 copy-done.7
  62.7 0.1 convert_divide_fusion
  62.8 0.0 copy-done.6
  62.8 0.1 copy.50
  62.9 24.2 %all_gather.10 = f32[2,1024,16]{2,0,1:T(2,128)S(1)} all-gather(f32[2,64,16]{2,0,1:T(2,128)S(1)} %copy.50), channel_id=1, replica_groups=mesh['groups'=2,'dev'=16] {'dev'}, dimensions={1}, use_global_device_ids=true | all-gather | bytes 139264 | tf_op jit(solution)/shard_map/all_gather | solution.py:74
  87.1 1.2 select_reduce_fusion
  88.3 1.1 fusion.49
  89.4 1.3 copy.65
  90.7 22.6 %all-gather.5.cloned.1.call-done = bf16[1024,2048]{1,0:T(8,128)(2,1)} async-done(((bf16[64,2048]{1,0:T(8,128)(2,1)}), bf16[1024,2048]{1,0:T(8,128)(2,1)}) %all-gather.5.cloned.1.call-update) | async-done | bytes 4194320 | tf_op jit(solution)/shard_map/all_gather | solution.py:86
  113.3 10.0 %fusion = f32[1024,1536]{1,0:T(8,128)S(1)} fusion(bf16[1024,2048]{1,0:T(8,128)(2,1)} %all-gather.5.cloned.1.call-done, bf16[1,2048,1536]{2,1,0:T(8,128)(2,1)} %param.12), kind=kOutput, calls=%fused_computation.8 | convolution fusion | flops 6442450944 | bytes 16777216 | tf_op jit(solution)/shard_map/dot_general | solution.py:55
  123.3 0.0 copy-done
  123.4 5.1 %multiply_convert_fusion = bf16[1024,2048]{1,0:T(8,128)(2,1)} fusion(f32[1024]{0:T(1024)S(1)} %bitcast.159, bf16[1,768,2048]{2,1,0:T(8,128)(2,1)S(1)} %copy-done, f32[1024,1536]{1,0:T(8,128)S(1)} %fusion), kind=kOutput, calls=%fused_computation | convolution fusion | flops 3230138368 | bytes 13635584 | tf_op jit(solution)/shard_map/dot_general | solution.py:59
  128.4 0.0 reduce-scatter.5.cloned.1.call-update
  128.5 0.0 reduce-scatter.3.cloned.1.call-start
  128.5 1.2 copy.63
  129.7 34.7 %all-gather.3.cloned.1.call-done = bf16[1024,2048]{1,0:T(8,128)(2,1)} async-done(((bf16[64,2048]{1,0:T(8,128)(2,1)}), bf16[1024,2048]{1,0:T(8,128)(2,1)}) %all-gather.3.cloned.1.call-update) | async-done | bytes 4194320 | tf_op jit(solution)/shard_map/all_gather | solution.py:86
  164.4 10.0 %fusion.2 = f32[1024,1536]{1,0:T(8,128)S(1)} fusion(bf16[1024,2048]{1,0:T(8,128)(2,1)} %all-gather.3.cloned.1.call-done, bf16[1,2048,1536]{2,1,0:T(8,128)(2,1)} %param.12), kind=kOutput, calls=%fused_computation.10 | convolution fusion | flops 6442450944 | bytes 16777216 | tf_op jit(solution)/shard_map/dot_general | solution.py:55
  174.4 5.1 %multiply_convert_fusion.1 = bf16[1024,2048]{1,0:T(8,128)(2,1)} fusion(f32[1024]{0:T(1024)S(1)} %bitcast.160, bf16[1,768,2048]{2,1,0:T(8,128)(2,1)S(1)} %copy-done, f32[1024,1536]{1,0:T(8,128)S(1)} %fusion.2), kind=kOutput, calls=%fused_computation.1 | convolution fusion | flops 3230138368 | bytes 13635584 | tf_op jit(solution)/shard_map/dot_general | solution.py:59
  179.5 0.0 reduce-scatter.3.cloned.1.call-update
  179.5 60.1 %reduce-scatter.5.cloned.1.call-done = bf16[64,2048]{1,0:T(8,128)(2,1)} async-done(((bf16[1024,2048]{1,0:T(8,128)(2,1)}), bf16[64,2048]{1,0:T(8,128)(2,1)}) %reduce-scatter.5.cloned.1.call-update) | async-done | bytes 262160 | tf_op jit(solution)/shard_map/reduce_scatter | solution.py:88
  239.6 75.5 %reduce-scatter.3.cloned.1.call-done = bf16[64,2048]{1,0:T(8,128)(2,1)} async-done(((bf16[1024,2048]{1,0:T(8,128)(2,1)}), bf16[64,2048]{1,0:T(8,128)(2,1)}) %reduce-scatter.3.cloned.1.call-update) | async-done | bytes 262160 | tf_op jit(solution)/shard_map/reduce_scatter | solution.py:88
  315.2 2.5 fusion.34
  (6 shorter events, 0.1 us)
Async XLA Ops:
  6.5 116.8 %copy-start = (bf16[1,768,2048]{2,1,0:T(8,128)(2,1)S(1)}, bf16[1,768,2048]{2,1,0:T(8,128)(2,1)}, u32[]{:S(2)}) copy-start(bf16[1,768,2048]{2,1,0:T(8,128)(2,1)} %param.13) | copy-start | bytes 9437188
  15.0 2.3 copy-start.3
  15.0 2.3 copy-start.4
  17.3 2.8 copy-start.1
  26.9 17.5 %all-to-all-start.1 = ((bf16[1,16,8,1024]{3,2,0,1:T(8,128)(2,1)}), bf16[1,16,8,1024]{3,2,0,1:T(8,128)(2,1)}, u32[]{:S(2)}, u32[]{:S(2)}) async-start(bf16[1,16,8,1024]{3,2,0,1:T(8,128)(2,1)} %bitcast.156), calls=%async_computation.2 | async-start | bytes 524288 | tf_op jit(solution)/shard_map/all_to_all | solution.py:83
  34.4 25.3 %copy-start.5 = (f32[2048]{0:T(1024)S(1)}, f32[2048]{0:T(1024)}, u32[]{:S(2)}) copy-start(f32[2048]{0:T(1024)} %param.11) | copy-start | bytes 24580
  39.9 22.8 %copy-start.7 = (s32[2,64,8]{1,2,0:T(8,128)S(1)}, s32[2,64,8]{1,2,0:T(8,128)}, u32[]{:S(2)}) copy-start(s32[2,64,8]{1,2,0:T(8,128)} %param.15) | copy-start | bytes 12292
  40.0 22.8 %copy-start.6 = (s32[2,64,8]{1,2,0:T(8,128)S(1)}, s32[2,64,8]{1,2,0:T(8,128)}, u32[]{:S(2)}) copy-start(s32[2,64,8]{1,2,0:T(8,128)} %param.14) | copy-start | bytes 12292
  44.5 13.5 %all-to-all-start = ((bf16[1,16,8,1024]{3,2,0,1:T(8,128)(2,1)}), bf16[1,16,8,1024]{3,2,0,1:T(8,128)(2,1)S(1)}, u32[]{:S(2)}, u32[]{:S(2)}) async-start(bf16[1,16,8,1024]{3,2,0,1:T(8,128)(2,1)} %bitcast.157), calls=%async_computation | async-start | bytes 524288 | tf_op jit(solution)/shard_map/all_to_all | solution.py:83
  48.0 65.3 %all-gather.5.cloned.1.call-start = ((), (), s32[]{:S(2)}) async-start(), calls=%async_computation.6 | async-start | bytes 4456448 | tf_op jit(solution)/shard_map/all_gather | solution.py:86
  58.1 1.7 copy-start.2
  61.9 102.5 %all-gather.3.cloned.1.call-start = ((), (), s32[]{:S(2)}) async-start(), calls=%async_computation.4 | async-start | bytes 4456448 | tf_op jit(solution)/shard_map/all_gather | solution.py:86
  62.7 177.0 %reduce-scatter.5.cloned.1.call-start = ((), (), s32[]{:S(2)}) async-start(), calls=%async_computation.7 | async-start | bytes 4456448 | tf_op jit(solution)/shard_map/reduce_scatter | solution.py:88
  128.5 186.7 %reduce-scatter.3.cloned.1.call-start = ((), (), s32[]{:S(2)}) async-start(), calls=%async_computation.5 | async-start | bytes 4456448 | tf_op jit(solution)/shard_map/reduce_scatter | solution.py:88
Sparse Core Ops, SparseCore 0:
  62.0 51.2 all-gather.4
  115.5 48.8 all-gather.2
  168.3 71.2 reduce-scatter.4
  243.3 71.7 reduce-scatter.2

commit v2 on v1

--- a/solution.py
+++ b/solution.py
@@ -1,8 +1,11 @@
+import functools
 import math
 
 import jax
 import jax.numpy as jnp
 from jax import lax
+from jax.experimental import pallas as pl
+from jax.experimental.pallas import tpu as pltpu
 from jax.sharding import PartitionSpec as P
 
 
@@ -60,6 +63,266 @@
     return (output * weight).astype(jnp.bfloat16)
 
 
+MESH = pl.DeviceIdType.MESH
+
+
+def moe_kernel(
+    chips, x_ref, w_ref, gu_hbm, dn_hbm, out_ref,
+    gathered, partial, pairbuf, ringbuf, gu, dn, xs, act,
+    load_sem, ag_send, ag_recv, agp_send, agp_recv, rsp_send, rsp_recv, rs_send, rs_recv,
+):
+    batches, rows, width = x_ref.shape
+    hidden = dn.shape[0]
+    far = chips // 2
+    me = lax.axis_index("dev")
+    core = me % 2
+    mine = me // 2
+    odd = mine % 2
+    pos = odd * ((mine + 1) // 2) + (1 - odd) * ((chips - mine // 2) % chips)
+
+    def chip_at(place):
+        q = (place + 2 * chips) % chips
+        upper = q // (far + 1)
+        some = (q + chips - 1) // chips
+        return some * ((1 - upper) * (2 * q - 1) + upper * 2 * (chips - q))
+
+    partner = mine * 2 + (1 - core)
+    ahead = (chip_at(pos + 1) * 2 + core, chip_at(pos - 1) * 2 + core)
+    sign = (1, -1)
+
+    def remote(src, dst, send, recv, target):
+        return pltpu.make_async_remote_copy(
+            src_ref=src, dst_ref=dst, send_sem=send, recv_sem=recv,
+            device_id={"dev": target}, device_id_type=MESH,
+        )
+
+    def ag_copy(way, dist, batch, origin, src=None):
+        slot = gathered.at[batch, origin, core]
+        return remote(
+            slot if src is None else src, slot,
+            ag_send.at[way, dist - 1, batch], ag_recv.at[way, dist - 1, batch], ahead[way],
+        )
+
+    def pair_copy(batch, origin, src=None):
+        slot = gathered.at[batch, origin, core]
+        return remote(
+            slot if src is None else src, slot,
+            agp_send.at[batch, origin], agp_recv.at[batch, origin], partner,
+        )
+
+    def pair_arrival(batch, origin):
+        slot = gathered.at[batch, origin, 1 - core]
+        return remote(slot, slot, agp_send.at[batch, origin], agp_recv.at[batch, origin], partner)
+
+    def sum_copy(batch, dest):
+        return remote(
+            partial.at[batch, dest, 1 - core], pairbuf.at[batch, dest],
+            rsp_send.at[batch, dest], rsp_recv.at[batch, dest], partner,
+        )
+
+    def rs_copy(way, turn, batch, dest):
+        return remote(
+            partial.at[batch, dest, core], ringbuf.at[way, turn, batch],
+            rs_send.at[way, turn, batch], rs_recv.at[way, turn, batch], ahead[way],
+        )
+
+    loads = (
+        pltpu.make_async_copy(gu_hbm.at[0], gu, load_sem.at[0]),
+        pltpu.make_async_copy(dn_hbm.at[0], dn, load_sem.at[1]),
+    )
+    for load in loads:
+        load.start()
+
+    barrier = pltpu.get_barrier_semaphore()
+    for target in (ahead[0], ahead[1], partner):
+        pl.semaphore_signal(barrier, inc=1, device_id={"dev": target}, device_id_type=MESH)
+    pl.semaphore_wait(barrier, 3)
+
+    for batch in range(batches):
+        for way in range(2):
+            ag_copy(way, 1, batch, mine, x_ref.at[batch]).start()
+    for batch in range(batches):
+        pair_copy(batch, mine, x_ref.at[batch]).start()
+        gathered[batch, mine, core] = x_ref[batch]
+    for load in loads:
+        load.wait()
+
+    tile = 256
+
+    def compute(blocks):
+        for at, (batch, chip, which) in enumerate(blocks):
+            xs[at * rows : (at + 1) * rows, :] = gathered[batch, chip, which]
+
+        @pl.loop(0, hidden // tile)
+        def _(j):
+            left = pl.ds(pl.multiple_of(j * tile, tile), tile)
+            right = pl.ds(pl.multiple_of(hidden + j * tile, tile), tile)
+            gate = jnp.dot(xs[...], gu[:, left], preferred_element_type=jnp.float32)
+            up = jnp.dot(xs[...], gu[:, right], preferred_element_type=jnp.float32)
+            act[:, left] = (gate / (1.0 + jnp.exp(-gate)) * up).astype(jnp.bfloat16)
+
+        @pl.loop(0, width // (2 * tile))
+        def _(j):
+            cols = pl.ds(pl.multiple_of(j * 2 * tile, 2 * tile), 2 * tile)
+            result = jnp.dot(act[...], dn[:, cols], preferred_element_type=jnp.float32)
+            for at, (batch, chip, which) in enumerate(blocks):
+                share = w_ref[batch, chip, which][:, :1]
+                piece = result[at * rows : (at + 1) * rows]
+                partial[batch, chip, which, :, cols] = (piece * share).astype(jnp.bfloat16)
+
+    for batch in range(batches):
+        pair_arrival(batch, mine).wait_recv()
+    compute([(batch, mine, which) for batch in range(batches) for which in range(2)])
+    for batch in range(batches):
+        sum_copy(batch, mine).start()
+
+    @pl.loop(0, 2 * (far - 1))
+    def _(step):
+        dist = step // 2 + 1
+        batch = step % 2
+        origins = (chip_at(pos - dist), chip_at(pos + dist))
+        for way in range(2):
+            ag_copy(way, dist, batch, origins[way]).wait_recv()
+
+            @pl.when((dist + 1 < far) | (batch == way))
+            def _():
+                ag_copy(way, dist + 1, batch, origins[way]).start()
+
+            pair_copy(batch, origins[way]).start()
+        for way in range(2):
+            pair_arrival(batch, origins[way]).wait_recv()
+        compute([(batch, origins[way], which) for way in range(2) for which in range(2)])
+        for way in range(2):
+            sum_copy(batch, origins[way]).start()
+
+    last = chip_at(pos + far)
+    for batch in range(batches):
+        ag_copy(batch, far, batch, last).wait_recv()
+        pair_copy(batch, last).start()
+    for batch in range(batches):
+        pair_arrival(batch, last).wait_recv()
+    compute([(batch, last, which) for batch in range(batches) for which in range(2)])
+    for batch in range(batches):
+        sum_copy(batch, last).start()
+
+    def gather_sum(batch, dest):
+        return partial[batch, dest, core].astype(jnp.float32) + pairbuf[batch, dest].astype(
+            jnp.float32
+        )
+
+    for batch in range(batches):
+        sum_copy(batch, last).wait_recv()
+        partial[batch, last, core] = gather_sum(batch, last).astype(jnp.bfloat16)
+        rs_copy(batch, 0, batch, last).start()
+
+    for way in range(2):
+        dest = chip_at(pos + sign[way] * (far - 1))
+        batch = 1 - way
+        sum_copy(batch, dest).wait_recv()
+        partial[batch, dest, core] = gather_sum(batch, dest).astype(jnp.bfloat16)
+        rs_copy(way, 1, batch, dest).start()
+    for way in range(2):
+        dest = chip_at(pos + sign[way] * (far - 1))
+        batch = way
+        sum_copy(batch, dest).wait_recv()
+        rs_copy(way, 0, batch, dest).wait_recv()
+        partial[batch, dest, core] = (
+            gather_sum(batch, dest) + ringbuf[way, 0, batch].astype(jnp.float32)
+        ).astype(jnp.bfloat16)
+        rs_copy(way, 1, batch, dest).start()
+
+    @pl.loop(0, 2 * (far - 2))
+    def _(step):
+        turn = step // 2 + 2
+        for way in range(2):
+            batch = (step + 1 + way) % 2
+            dest = chip_at(pos + sign[way] * (far - turn))
+            sum_copy(batch, dest).wait_recv()
+            rs_copy(way, turn - 1, batch, dest).wait_recv()
+            partial[batch, dest, core] = (
+                gather_sum(batch, dest) + ringbuf[way, turn - 1, batch].astype(jnp.float32)
+            ).astype(jnp.bfloat16)
+            rs_copy(way, turn, batch, dest).start()
+
+    for batch in range(batches):
+        sum_copy(batch, mine).wait_recv()
+    for way in range(2):
+        rs_copy(way, far - 1, 1 - way, mine).wait_recv()
+    for way in range(2):
+        rs_copy(way, far - 1, way, mine).wait_recv()
+    for batch in range(batches):
+        out_ref[batch] = (
+            gather_sum(batch, mine)
+            + ringbuf[0, far - 1, batch].astype(jnp.float32)
+            + ringbuf[1, far - 1, batch].astype(jnp.float32)
+        )
+
+    for way in range(2):
+        for batch in range(batches):
+            ag_copy(way, 1, batch, mine, x_ref.at[batch]).wait_send()
+        ag_copy(way, far, way, mine).wait_send()
+
+        @pl.loop(0, 2 * (far - 2))
+        def _(step):
+            ag_copy(way, step // 2 + 2, step % 2, mine).wait_send()
+
+        rs_copy(way, 0, way, mine).wait_send()
+
+        @pl.loop(0, 2 * (far - 1))
+        def _(step):
+            rs_copy(way, step // 2 + 1, step % 2, mine).wait_send()
+
+    @pl.loop(0, 2 * chips)
+    def _(step):
+        pair_copy(step % 2, step // 2).wait_send()
+        sum_copy(step % 2, step // 2).wait_send()
+
+
+def fits(devices, rows, width, hidden):
+    block = 2 * rows * width * 2
+    needed = devices * block * 2 + devices // 2 * block + devices // 2 * block
+    needed += 3 * width * hidden * 2 + 4 * rows * width * 2 + devices * rows * 2 * 512
+    return devices % 4 == 0 and devices >= 8 and needed < 46 * 1024 * 1024
+
+
+def routed_experts(normed, weights, gate_up, down_proj, devices):
+    batches, rows, width = normed.shape
+    hidden = down_proj.shape[1]
+    chips = devices // 2
+    far = chips // 2
+    dma = pltpu.SemaphoreType.DMA
+    spread = jnp.broadcast_to(
+        weights.reshape(batches, chips, 2, rows, 1), (batches, chips, 2, rows, 128)
+    )
+    vmem = pl.BlockSpec(memory_space=pltpu.VMEM)
+    anywhere = pl.BlockSpec(memory_space=pl.ANY)
+    kind = jnp.bfloat16
+    return pl.pallas_call(
+        functools.partial(moe_kernel, chips),
+        out_shape=jax.ShapeDtypeStruct((batches, rows, width), jnp.float32),
+        in_specs=[vmem, vmem, anywhere, anywhere],
+        out_specs=vmem,
+        scratch_shapes=[
+            pltpu.VMEM((batches, chips, 2, rows, width), kind),
+            pltpu.VMEM((batches, chips, 2, rows, width), kind),
+            pltpu.VMEM((batches, chips, rows, width), kind),
+            pltpu.VMEM((2, far, batches, rows, width), kind),
+            pltpu.VMEM((width, 2 * hidden), kind),
+            pltpu.VMEM((hidden, width), kind),
+            pltpu.VMEM((4 * rows, width), kind),
+            pltpu.VMEM((4 * rows, hidden), kind),
+            dma((2,)),
+            dma((2, far, batches)), dma((2, far, batches)),
+            dma((batches, chips)), dma((batches, chips)),
+            dma((batches, chips)), dma((batches, chips)),
+            dma((2, far, batches)), dma((2, far, batches)),
+        ],
+        compiler_params=pltpu.CompilerParams(
+            collective_id=0, has_side_effects=True, vmem_limit_bytes=56 * 1024 * 1024
+        ),
+    )(normed, spread, gate_up, down_proj)
+
+
 def body(queries, keys_values, residual, norm_gain, gate_up, down_proj, expert_ids, expert_gates):
     devices = lax.axis_size("dev")
     me = lax.axis_index("dev")
@@ -75,7 +338,7 @@
     mine = jnp.sum(
         jnp.where(jnp.arange(experts, dtype=jnp.int32) == me, weights, 0.0), axis=-1, keepdims=True
     )
-    pieces = []
+    streams, rows_out = [], []
     for batch_index in range(batches):
         window = slice(batch_index, batch_index + 1)
         blended_heads = attend(own_query[window], own_pairs[window])
@@ -83,10 +346,17 @@
         arrived_rows = lax.all_to_all(outgoing_rows, "dev", split_axis=1, concat_axis=1, tiled=True)
         attn_rows = to_owners(arrived_rows, kv_heads)
         stream, normed = prepare(attn_rows[0], residual[batch_index], norm_gain)
-        rows_in = lax.all_gather(normed, "dev", axis=0, tiled=True)
+        streams.append(stream)
+        rows_out.append(normed)
+    if batches == 2 and fits(devices, residual.shape[1], model_width, down_proj.shape[1]):
+        summed = routed_experts(jnp.stack(rows_out), mine, gate_up, down_proj, devices)
+        return (jnp.stack(streams) + summed).astype(jnp.bfloat16)
+    pieces = []
+    for batch_index in range(batches):
+        rows_in = lax.all_gather(rows_out[batch_index], "dev", axis=0, tiled=True)
         partial = run_expert(rows_in, gate_up, down_proj, mine[batch_index])
         summed = lax.psum_scatter(partial, "dev", scatter_dimension=0, tiled=True)
-        pieces.append((stream + summed.astype(jnp.float32)).astype(jnp.bfloat16))
+        pieces.append((streams[batch_index] + summed.astype(jnp.float32)).astype(jnp.bfloat16))
     return jnp.stack(pieces, axis=0)
 
 

time: 325 us -> 166 us (0.51)
  waiting for transfers between devices: 205 us -> 1.47 us
  Pallas kernels: 0 us -> 99.4 us
  matrix products: 43.3 us -> 10.9 us
  between operations: 13.4 us -> 0.2 us
  local copies, waits for them, and re-layouts: 15.7 us -> 6.73 us
    reduce_scatter x2 -> x0, waiting for transfers between devices: 136 us -> none  [body(): summed = lax.psum_scatter(partial, 'dev', scatter_dimension=0, tiled=True)]
    pallas_call x0 -> x1, Pallas kernels: none -> 99.4 us  [routed_experts(): pl.pallas_call(functools.partial(moe_kernel, chips), out_shape=jax.ShapeD...]
    all_gather x2 -> x0, waiting for transfers between devices: 57.3 us -> none  [body(): rows_in = lax.all_gather(normed, 'dev', axis=0, tiled=True)]
    dot_general x4 -> x0, matrix products: 30.2 us -> none  [the longest x2 20 us: run_expert(): projected = jnp.dot(rows_in, gate_up[0], preferred_element_type=jnp.float32)]
    all_to_all x2, waiting for transfers between devices: 11.4 us -> 1.47 us  [body(): lax.all_to_all(outgoing_rows, 'dev', split_axis=1, concat_axis=1, tiled=T...]
    unnamed x20 -> x12, local copies, waits for them, and re-layouts: 6.13 us -> 0.53 us
  transfers between devices with their start and end apart: 6 -> 2, of which waited for: 6 -> 1; matrix products, arithmetic and copies ran while one was open for 13% -> 6% of each run, Pallas kernels for 0% -> 0%
where the time goes in v2:
time: 166 us; the launch traced here: 165 us
  Pallas kernels  99.4 us (60%)
  blocking collectives  24.9 us (15%)
  starting transfers between devices  12 us (7%)
  matrix products  10.9 us (7%)
  other arithmetic  9.61 us (6%)
  local copies, waits for them, and re-layouts  6.73 us (4%)
    pallas_call x1, Pallas kernels, routed_experts(): pl.pallas_call(functools.partial(moe_kernel, chips), out_shape=jax.ShapeD...  99.4 us
    all_gather x1, blocking collectives, body(): weights = lax.all_gather(weights, 'dev', axis=1, tiled=True)  24.9 us
    all_to_all x2, starting transfers between devices, body(): lax.all_to_all(outgoing_rows, 'dev', split_axis=1, concat_axis=1, tiled=T...  12 us
    dot_general x2, matrix products, attend(): jnp.einsum('mqgd,mkd->mgqk', head_rows, cached_pairs[:, 0], preferred_ele...  5.78 us
    dot_general x2, matrix products, attend(): jnp.einsum('mgqk,mkd->mqgd', weights, cached_pairs[:, 1], preferred_eleme...  5.15 us
    reduce_sum x1, other arithmetic, attend(): totals = jnp.sum(scaled_exp, axis=-1, keepdims=True)  4.69 us
  transfers between devices with their start and end apart: 2, of which 1 were waited for; matrix products, arithmetic and copies ran while one was open for 6% of the time, Pallas kernels for 0%

profile of v2, /device:TPU:0, one launch (start us, length us, event | category | flops | bytes accessed | tf_op | source)
XLA Modules:
  0.0 165.2 jit_solution(16272345667868732067)
XLA Ops:
  0.0 0.1 iota_compare_fusion
  0.2 1.1 fusion.40
  1.2 0.2 copy.62
  1.4 1.5 slice_bitcast_fusion
  2.9 0.2 copy.63
  3.1 1.1 fusion
  4.2 4.7 %fusion.2 = (f32[8,128]{1,0:T(8,128)S(1)}, f32[8,128]{1,0:T(8,128)S(1)}, f32[1664,128,8]{1,0,2:T(8,128)}) fusion(f32[1664,128,8]{1,0,2:T(8,128)S(1)} %get-tuple-element.20, f32[8,128]{1,0:T(8,128)S(1)} %get-tuple-element.19, pred[128,1664]{0,1:T(8,128)(4,1)S(1)} %iota_compare_fusion, bf16[128,8,128]{0,2,1:T(8,128)(2,1)S(1)} %bitcast.141, ...), kind=kOutput, calls=%fused_computation.8 | convolution fusion | flops 449837056 | bytes 14544896 | tf_op jit(solution)/shard_map/mqgd,mkd->mgqk/dot_general | solution.py:18
  8.9 2.6 %fusion.17 = bf16[1,128,8,128]{3,1,2,0:T(8,128)(2,1)S(1)} fusion(f32[8,128]{1,0:T(8,128)S(1)} %get-tuple-element.7, f32[8,128]{1,0:T(8,128)S(1)} %get-tuple-element.19, f32[1664,128,8]{1,0,2:T(8,128)S(1)} %get-tuple-element.20, pred[128,1664]{0,1:T(8,128)(4,1)S(1)} %iota_compare_fusion, bf16[1,2,1664,128]{3,2,1,0:T(8,128)(2,1)S(1)} %get-tuple-element.14), kind=kOutput, calls=%fused_computation.17 | convolution fusion | flops 446562304 | bytes 7725056 | tf_op jit(solution)/shard_map/mgqk,mkd->mqgd/dot_general | solution.py:29
  11.5 0.2 copy.48
  11.6 0.8 reshape_reshape.6
  12.5 7.4 %all-to-all-start = ((bf16[1,16,8,1024]{3,2,0,1:T(8,128)(2,1)}), bf16[1,16,8,1024]{3,2,0,1:T(8,128)(2,1)S(1)}, u32[]{:S(2)}, u32[]{:S(2)}) async-start(bf16[1,16,8,1024]{3,2,0,1:T(8,128)(2,1)} %bitcast.12), calls=%async_computation | async-start | bytes 524288 | tf_op jit(solution)/shard_map/all_to_all | solution.py:346
  19.9 0.0 copy-start
  19.9 4.7 %fusion.3 = f32[8,128]{1,0:T(8,128)S(1)} fusion(f32[1664,128,8]{1,0,2:T(8,128)} %get-tuple-element.21, f32[8,128]{1,0:T(8,128)S(1)} %get-tuple-element.8, pred[128,1664]{0,1:T(8,128)(4,1)S(1)} %iota_compare_fusion), kind=kLoop, calls=%fused_computation.9 | loop fusion | flops 8518656 | bytes 7036928 | tf_op jit(solution)/shard_map/reduce_sum | solution.py:27
  24.6 0.2 copy-done
  24.8 0.0 copy-start.4
  24.8 0.0 copy-start.3
  24.8 2.6 %fusion.14 = bf16[1,128,8,128]{3,1,2,0:T(8,128)(2,1)S(1)} fusion(f32[8,128]{1,0:T(8,128)S(1)} %fusion.3, f32[8,128]{1,0:T(8,128)S(1)} %get-tuple-element.8, f32[1664,128,8]{1,0,2:T(8,128)S(1)} %copy-done, pred[128,1664]{0,1:T(8,128)(4,1)S(1)} %iota_compare_fusion, bf16[1,2,1664,128]{3,2,1,0:T(8,128)(2,1)S(1)} %get-tuple-element.13), kind=kOutput, calls=%fused_computation.16 | convolution fusion | flops 446562304 | bytes 7725056 | tf_op jit(solution)/shard_map/mgqk,mkd->mqgd/dot_general | solution.py:29
  27.4 0.0 copy-start.1
  27.4 0.0 copy-start.2
  27.4 0.2 copy.53
  27.6 0.8 reshape_reshape.7
  28.4 0.0 copy-done.4
  28.4 1.5 all-to-all-done
  29.9 4.6 %all-to-all-start.1 = ((bf16[1,16,8,1024]{3,2,0,1:T(8,128)(2,1)}), bf16[1,16,8,1024]{3,2,0,1:T(8,128)(2,1)S(1)}, u32[]{:S(2)}, u32[]{:S(2)}) async-start(bf16[1,16,8,1024]{3,2,0,1:T(8,128)(2,1)} %bitcast.28), calls=%async_computation.1 | async-start | bytes 524288 | tf_op jit(solution)/shard_map/all_to_all | solution.py:346
  34.5 0.0 copy-done.3
  34.5 0.1 copy.55
  34.6 24.9 %all_gather.3 = f32[2,1024,16]{2,0,1:T(2,128)S(1)} all-gather(f32[2,64,16]{2,0,1:T(2,128)S(1)} %copy.55), channel_id=1, replica_groups=mesh['groups'=2,'dev'=16] {'dev'}, dimensions={1}, use_global_device_ids=true | all-gather | bytes 139264 | tf_op jit(solution)/shard_map/all_gather | solution.py:337
  59.5 1.2 select_reduce_fusion
  60.7 0.2 copy.64
  60.9 0.1 convert.14
  61.0 0.0 all-to-all-done.1
  61.0 0.0 copy-done.1
  61.0 0.2 fusion.23
  61.3 0.0 copy-done.2
  61.3 0.2 multiply_convert_fusion.1
  61.5 0.8 pad_maximum_fusion.x_ref
  62.3 1.3 broadcast_in_dim.69.w_ref
  63.7 99.4 %shard_map.82 = f32[2,64,2048]{2,1,0:T(8,128)} custom-call(bf16[2,64,2048]{2,1,0:T(8,128)(2,1)} %pad_maximum_fusion.x_ref, f32[2,8,2,64,128]{4,3,2,1,0:T(8,128)} %broadcast_in_dim.69.w_ref, bf16[1,2048,1536]{2,1,0:T(8,128)(2,1)} %gu_hbm.1, bf16[1,768,2048]{2,1,0:T(8,128)(2,1)} %dn_hbm.1), custom_call_target="tpu_custom_call" | custom-call | tf_op jit(solution)/shard_map/pallas_call | solution.py:300
  163.1 2.1 %fusion.20 = bf16[2,64,2048]{2,1,0:T(8,128)(2,1)} fusion(f32[2,64,2048]{2,1,0:T(8,128)} %shard_map.82, f32[1,64,2048]{2,1,0:T(8,128)S(1)} %get-tuple-element.16, f32[1,64,2048]{2,1,0:T(8,128)S(1)} %get-tuple-element.10), kind=kLoop, calls=%fused_computation.19 | loop fusion | flops 786432 | bytes 2621440 | tf_op jit(solution)/shard_map/convert_element_type | solution.py:353
  (6 shorter events, 0.1 us)
Async XLA Ops:
  12.5 17.4 %all-to-all-start = ((bf16[1,16,8,1024]{3,2,0,1:T(8,128)(2,1)}), bf16[1,16,8,1024]{3,2,0,1:T(8,128)(2,1)S(1)}, u32[]{:S(2)}, u32[]{:S(2)}) async-start(bf16[1,16,8,1024]{3,2,0,1:T(8,128)(2,1)} %bitcast.12), calls=%async_computation | async-start | bytes 524288 | tf_op jit(solution)/shard_map/all_to_all | solution.py:346
  19.9 4.9 %copy-start = (f32[1664,128,8]{1,0,2:T(8,128)S(1)}, f32[1664,128,8]{1,0,2:T(8,128)}, u32[]{:S(2)}) copy-start(f32[1664,128,8]{1,0,2:T(8,128)} %get-tuple-element.21) | copy-start | bytes 20447236
  24.8 3.6 %copy-start.4 = (s32[2,64,8]{1,2,0:T(8,128)S(1)}, s32[2,64,8]{1,2,0:T(8,128)}, u32[]{:S(2)}) copy-start(s32[2,64,8]{1,2,0:T(8,128)} %param.15) | copy-start | bytes 12292
  24.8 9.7 %copy-start.3 = (s32[2,64,8]{1,2,0:T(8,128)S(1)}, s32[2,64,8]{1,2,0:T(8,128)}, u32[]{:S(2)}) copy-start(s32[2,64,8]{1,2,0:T(8,128)} %param.14) | copy-start | bytes 12292
  27.4 33.7 %copy-start.1 = (bf16[2,64,2048]{2,1,0:T(8,128)(2,1)S(1)}, bf16[2,64,2048]{2,1,0:T(8,128)(2,1)}, u32[]{:S(2)}) copy-start(bf16[2,64,2048]{2,1,0:T(8,128)(2,1)} %param.10) | copy-start | bytes 1572868
  27.4 33.9 %copy-start.2 = (f32[2048]{0:T(1024)S(1)}, f32[2048]{0:T(1024)}, u32[]{:S(2)}) copy-start(f32[2048]{0:T(1024)} %param.11) | copy-start | bytes 24580
  29.9 31.1 %all-to-all-start.1 = ((bf16[1,16,8,1024]{3,2,0,1:T(8,128)(2,1)}), bf16[1,16,8,1024]{3,2,0,1:T(8,128)(2,1)S(1)}, u32[]{:S(2)}, u32[]{:S(2)}) async-start(bf16[1,16,8,1024]{3,2,0,1:T(8,128)(2,1)} %bitcast.28), calls=%async_computation.1 | async-start | bytes 524288 | tf_op jit(solution)/shard_map/all_to_all | solution.py:346

commit v3 on v2

--- a/solution.py
+++ b/solution.py
@@ -67,11 +67,13 @@
 
 
 def moe_kernel(
-    chips, x_ref, w_ref, gu_hbm, dn_hbm, out_ref,
-    gathered, partial, pairbuf, ringbuf, gu, dn, xs, act,
-    load_sem, ag_send, ag_recv, agp_send, agp_recv, rsp_send, rsp_recv, rs_send, rs_recv,
+    chips, heads_ref, res_ref, gain_ref, share_ref, gu_hbm, dn_hbm, out_ref,
+    attn, stream, gathered, partial, pairbuf, ringbuf, gu, dn, xs, sh, act,
+    load_sem, ex_send, ex_recv, ag_send, ag_recv, agp_send, agp_recv, rsp_send, rsp_recv, rs_send, rs_recv,
 ):
-    batches, rows, width = x_ref.shape
+    batches, rows, width = res_ref.shape
+    devices = 2 * chips
+    kv_heads, part = attn.shape[2], attn.shape[4]
     hidden = dn.shape[0]
     far = chips // 2
     me = lax.axis_index("dev")
@@ -96,19 +98,16 @@
             device_id={"dev": target}, device_id_type=MESH,
         )
 
-    def ag_copy(way, dist, batch, origin, src=None):
+    def ag_copy(way, dist, batch, origin):
         slot = gathered.at[batch, origin, core]
         return remote(
-            slot if src is None else src, slot,
+            slot, slot,
             ag_send.at[way, dist - 1, batch], ag_recv.at[way, dist - 1, batch], ahead[way],
         )
 
-    def pair_copy(batch, origin, src=None):
+    def pair_copy(batch, origin):
         slot = gathered.at[batch, origin, core]
-        return remote(
-            slot if src is None else src, slot,
-            agp_send.at[batch, origin], agp_recv.at[batch, origin], partner,
-        )
+        return remote(slot, slot, agp_send.at[batch, origin], agp_recv.at[batch, origin], partner)
 
     def pair_arrival(batch, origin):
         slot = gathered.at[batch, origin, 1 - core]
@@ -125,6 +124,16 @@
             partial.at[batch, dest, core], ringbuf.at[way, turn, batch],
             rs_send.at[way, turn, batch], rs_recv.at[way, turn, batch], ahead[way],
         )
+
+    def exchange(batch, target):
+        return remote(
+            heads_ref.at[batch, target], attn.at[batch, me // kv_heads, me % kv_heads],
+            ex_send.at[batch, target], ex_recv.at[batch, me], target,
+        )
+
+    def arrival(batch, source):
+        slot = attn.at[batch, source // kv_heads, source % kv_heads]
+        return remote(slot, slot, ex_send.at[batch, source], ex_recv.at[batch, source], source)
 
     loads = (
         pltpu.make_async_copy(gu_hbm.at[0], gu, load_sem.at[0]),
@@ -134,16 +143,42 @@
         load.start()
 
     barrier = pltpu.get_barrier_semaphore()
-    for target in (ahead[0], ahead[1], partner):
+
+    @pl.loop(1, devices)
+    def _(k):
+        target = (me + k) % devices
         pl.semaphore_signal(barrier, inc=1, device_id={"dev": target}, device_id_type=MESH)
-    pl.semaphore_wait(barrier, 3)
-
-    for batch in range(batches):
+
+    pl.semaphore_wait(barrier, devices - 1)
+
+    for batch in range(batches):
+
+        @pl.loop(1, devices)
+        def _(k):
+            exchange(batch, (me + k) % devices).start()
+
+    for batch in range(batches):
+        attn[batch, me // kv_heads, me % kv_heads] = heads_ref[batch, me]
+        gathered[batch, mine, core, :, width:] = share_ref[batch]
+
+        @pl.loop(1, devices)
+        def _(k):
+            arrival(batch, (me + k) % devices).wait_recv()
+
+        squares = jnp.zeros((rows, 1), jnp.float32)
+        for head in range(kv_heads):
+            cols = slice(head * part, (head + 1) * part)
+            added = attn[batch, :, head].astype(jnp.float32).reshape(rows, part)
+            added = added + res_ref[batch, :, cols].astype(jnp.float32)
+            stream[batch, :, cols] = added
+            squares = squares + jnp.sum(added * added, axis=-1, keepdims=True)
+        scale = lax.rsqrt(squares / width + 1e-06)
+        gathered[batch, mine, core, :, :width] = (
+            stream[batch] * scale * gain_ref[...]
+        ).astype(jnp.bfloat16)
         for way in range(2):
-            ag_copy(way, 1, batch, mine, x_ref.at[batch]).start()
-    for batch in range(batches):
-        pair_copy(batch, mine, x_ref.at[batch]).start()
-        gathered[batch, mine, core] = x_ref[batch]
+            ag_copy(way, 1, batch, mine).start()
+        pair_copy(batch, mine).start()
     for load in loads:
         load.wait()
 
@@ -151,7 +186,12 @@
 
     def compute(blocks):
         for at, (batch, chip, which) in enumerate(blocks):
-            xs[at * rows : (at + 1) * rows, :] = gathered[batch, chip, which]
+            xs[at * rows : (at + 1) * rows, :] = gathered[batch, chip, which, :, :width]
+            lanes = gathered[batch, chip, which, :, width:].astype(jnp.float32)
+            lane = lax.broadcasted_iota(jnp.int32, lanes.shape, 1)
+            mask = (lane == me) | (lane == me + devices)
+            share = jnp.sum(jnp.where(mask, lanes, 0.0), axis=-1, keepdims=True)
+            sh[at * rows : (at + 1) * rows, :] = jnp.broadcast_to(share, lanes.shape)
 
         @pl.loop(0, hidden // tile)
         def _(j):
@@ -166,7 +206,7 @@
             cols = pl.ds(pl.multiple_of(j * 2 * tile, 2 * tile), 2 * tile)
             result = jnp.dot(act[...], dn[:, cols], preferred_element_type=jnp.float32)
             for at, (batch, chip, which) in enumerate(blocks):
-                share = w_ref[batch, chip, which][:, :1]
+                share = sh[at * rows : (at + 1) * rows, :1]
                 piece = result[at * rows : (at + 1) * rows]
                 partial[batch, chip, which, :, cols] = (piece * share).astype(jnp.bfloat16)
 
@@ -252,14 +292,22 @@
         rs_copy(way, far - 1, way, mine).wait_recv()
     for batch in range(batches):
         out_ref[batch] = (
-            gather_sum(batch, mine)
-            + ringbuf[0, far - 1, batch].astype(jnp.float32)
-            + ringbuf[1, far - 1, batch].astype(jnp.float32)
-        )
+            stream[batch]
+            + (
+                gather_sum(batch, mine)
+                + ringbuf[0, far - 1, batch].astype(jnp.float32)
+                + ringbuf[1, far - 1, batch].astype(jnp.float32)
+            )
+        ).astype(out_ref.dtype)
+
+    @pl.loop(1, devices)
+    def _(k):
+        for batch in range(batches):
+            exchange(batch, (me + k) % devices).wait_send()
 
     for way in range(2):
         for batch in range(batches):
-            ag_copy(way, 1, batch, mine, x_ref.at[batch]).wait_send()
+            ag_copy(way, 1, batch, mine).wait_send()
         ag_copy(way, far, way, mine).wait_send()
 
         @pl.loop(0, 2 * (far - 2))
@@ -279,39 +327,48 @@
 
 
 def fits(devices, rows, width, hidden):
-    block = 2 * rows * width * 2
-    needed = devices * block * 2 + devices // 2 * block + devices // 2 * block
-    needed += 3 * width * hidden * 2 + 4 * rows * width * 2 + devices * rows * 2 * 512
-    return devices % 4 == 0 and devices >= 8 and needed < 46 * 1024 * 1024
-
-
-def routed_experts(normed, weights, gate_up, down_proj, devices):
-    batches, rows, width = normed.shape
+    block = 2 * rows * (width + 128) * 2
+    needed = 3 * devices * block + 3 * width * hidden * 2 + 8 * rows * width * 4
+    return devices % 4 == 0 and 8 <= devices <= 64 and needed < 48 * 1024 * 1024
+
+
+def share_lanes(weights):
+    coarse = lax.reduce_precision(weights, 8, 7)
+    fine = lax.reduce_precision(weights - coarse, 8, 7)
+    both = jnp.concatenate([coarse, fine], axis=-1)
+    gap = 128 - both.shape[-1]
+    return jnp.pad(both, ((0, 0), (0, 0), (0, gap))).astype(jnp.bfloat16)
+
+
+def routed_layer(heads, residual, norm_gain, lanes, gate_up, down_proj, kv_heads):
+    batches, rows, width = residual.shape
+    devices, span, part = heads.shape[1:]
     hidden = down_proj.shape[1]
     chips = devices // 2
     far = chips // 2
     dma = pltpu.SemaphoreType.DMA
-    spread = jnp.broadcast_to(
-        weights.reshape(batches, chips, 2, rows, 1), (batches, chips, 2, rows, 128)
-    )
     vmem = pl.BlockSpec(memory_space=pltpu.VMEM)
     anywhere = pl.BlockSpec(memory_space=pl.ANY)
     kind = jnp.bfloat16
     return pl.pallas_call(
         functools.partial(moe_kernel, chips),
-        out_shape=jax.ShapeDtypeStruct((batches, rows, width), jnp.float32),
-        in_specs=[vmem, vmem, anywhere, anywhere],
+        out_shape=jax.ShapeDtypeStruct((batches, rows, width), kind),
+        in_specs=[vmem, vmem, vmem, vmem, anywhere, anywhere],
         out_specs=vmem,
         scratch_shapes=[
-            pltpu.VMEM((batches, chips, 2, rows, width), kind),
+            pltpu.VMEM((batches, devices // kv_heads, kv_heads, span, part), kind),
+            pltpu.VMEM((batches, rows, width), jnp.float32),
+            pltpu.VMEM((batches, chips, 2, rows, width + 128), kind),
             pltpu.VMEM((batches, chips, 2, rows, width), kind),
             pltpu.VMEM((batches, chips, rows, width), kind),
             pltpu.VMEM((2, far, batches, rows, width), kind),
             pltpu.VMEM((width, 2 * hidden), kind),
             pltpu.VMEM((hidden, width), kind),
             pltpu.VMEM((4 * rows, width), kind),
+            pltpu.VMEM((4 * rows, 128), jnp.float32),
             pltpu.VMEM((4 * rows, hidden), kind),
             dma((2,)),
+            dma((batches, devices)), dma((batches, devices)),
             dma((2, far, batches)), dma((2, far, batches)),
             dma((batches, chips)), dma((batches, chips)),
             dma((batches, chips)), dma((batches, chips)),
@@ -320,7 +377,7 @@
         compiler_params=pltpu.CompilerParams(
             collective_id=0, has_side_effects=True, vmem_limit_bytes=56 * 1024 * 1024
         ),
-    )(normed, spread, gate_up, down_proj)
+    )(heads, residual, norm_gain.reshape(1, width), lanes, gate_up, down_proj)
 
 
 def body(queries, keys_values, residual, norm_gain, gate_up, down_proj, expert_ids, expert_gates):
@@ -334,29 +391,28 @@
     batches, length, feat_width = own_query.shape
     positions = length // devices
     weights = dense_shares(expert_ids, expert_gates, experts)
+    blended = [
+        attend(own_query[index : index + 1], own_pairs[index : index + 1])
+        for index in range(batches)
+    ]
+    if batches == 2 and fits(devices, residual.shape[1], model_width, down_proj.shape[1]):
+        heads = jnp.concatenate(blended).reshape(batches, devices, positions, feat_width)
+        lanes = share_lanes(weights)
+        return routed_layer(heads, residual, norm_gain, lanes, gate_up, down_proj, kv_heads)
     weights = lax.all_gather(weights, "dev", axis=1, tiled=True)
     mine = jnp.sum(
         jnp.where(jnp.arange(experts, dtype=jnp.int32) == me, weights, 0.0), axis=-1, keepdims=True
     )
-    streams, rows_out = [], []
+    pieces = []
     for batch_index in range(batches):
-        window = slice(batch_index, batch_index + 1)
-        blended_heads = attend(own_query[window], own_pairs[window])
-        outgoing_rows = blended_heads.reshape(1, devices, positions, feat_width)
+        outgoing_rows = blended[batch_index].reshape(1, devices, positions, feat_width)
         arrived_rows = lax.all_to_all(outgoing_rows, "dev", split_axis=1, concat_axis=1, tiled=True)
         attn_rows = to_owners(arrived_rows, kv_heads)
         stream, normed = prepare(attn_rows[0], residual[batch_index], norm_gain)
-        streams.append(stream)
-        rows_out.append(normed)
-    if batches == 2 and fits(devices, residual.shape[1], model_width, down_proj.shape[1]):
-        summed = routed_experts(jnp.stack(rows_out), mine, gate_up, down_proj, devices)
-        return (jnp.stack(streams) + summed).astype(jnp.bfloat16)
-    pieces = []
-    for batch_index in range(batches):
-        rows_in = lax.all_gather(rows_out[batch_index], "dev", axis=0, tiled=True)
+        rows_in = lax.all_gather(normed, "dev", axis=0, tiled=True)
         partial = run_expert(rows_in, gate_up, down_proj, mine[batch_index])
         summed = lax.psum_scatter(partial, "dev", scatter_dimension=0, tiled=True)
-        pieces.append((streams[batch_index] + summed.astype(jnp.float32)).astype(jnp.bfloat16))
+        pieces.append((stream + summed.astype(jnp.float32)).astype(jnp.bfloat16))
     return jnp.stack(pieces, axis=0)
 
 

time: 166 us -> 146 us (0.88)
  blocking collectives: 24.9 us -> 0 us
  Pallas kernels: 99.4 us -> 116 us
  starting transfers between devices: 12 us -> 0 us
  matrix products: 10.9 us -> 16.1 us
  other arithmetic: 9.61 us -> 6.44 us
    all_gather x1 -> x0, blocking collectives: 24.9 us -> none  [body(): weights = lax.all_gather(weights, 'dev', axis=1, tiled=True)]
    pallas_call x1, Pallas kernels: 99.4 us -> 116 us  [routed_layer(): pl.pallas_call(functools.partial(moe_kernel, chips), out_shape=jax.ShapeD...]
    all_to_all x2 -> x0, starting transfers between devices: 12 us -> none  [body(): lax.all_to_all(outgoing_rows, 'dev', split_axis=1, concat_axis=1, tiled=T...]
    dot_general x2, matrix products: 5.78 us -> 11 us  [attend(): jnp.einsum('mqgd,mkd->mgqk', head_rows, cached_pairs[:, 0], preferred_ele...]
    convert_element_type x4 -> x0, other arithmetic: 2.44 us -> none  [the longest x1 2.14 us: body(): return (jnp.stack(streams) + summed).astype(jnp.bfloat16)]
    unnamed x12 -> x19, local copies, waits for them, and re-layouts: 0.53 us -> 2.47 us
  transfers between devices with their start and end apart: 2 -> 0, of which waited for: 1 -> 0; matrix products, arithmetic and copies ran while one was open for 6% -> 0% of each run, Pallas kernels for 0% -> 0%
where the time goes in v3:
time: 146 us
  Pallas kernels  116 us (79%)
  matrix products  16.1 us (11%)
  local copies, waits for them, and re-layouts  7.06 us (5%)
  other arithmetic  6.44 us (4%)
    pallas_call x1, Pallas kernels, routed_layer(): pl.pallas_call(functools.partial(moe_kernel, chips), out_shape=jax.ShapeD...  116 us
    dot_general x2, matrix products, attend(): jnp.einsum('mqgd,mkd->mgqk', head_rows, cached_pairs[:, 0], preferred_ele...  11 us
    dot_general x2, matrix products, attend(): jnp.einsum('mgqk,mkd->mqgd', weights, cached_pairs[:, 1], preferred_eleme...  5.15 us
    reduce_sum x1, other arithmetic, attend(): totals = jnp.sum(scaled_exp, axis=-1, keepdims=True)  4.69 us

profile of v3, /device:TPU:0, one launch (start us, length us, event | category | flops | bytes accessed | tf_op | source)
XLA Modules:
  0.0 146.1 jit_solution(5678814165324424708)
XLA Ops:
  0.0 0.1 iota_compare_fusion
  0.2 2.5 %slice_bitcast_fusion.1 = (bf16[1,2,1664,128]{3,2,1,0:T(8,128)(2,1)S(1)}, bf16[1,2,1664,128]{3,2,1,0:T(8,128)(2,1)}) fusion(bf16[2,1,2,1664,128]{4,3,2,1,0:T(8,128)(2,1)} %param.9), kind=kLoop, calls=%fused_computation.19 | loop fusion | bytes 3407872 | tf_op jit(solution)/shard_map/slice | solution.py:395
  2.6 0.0 copy-start.1
  2.6 1.4 fusion.36
  4.0 0.2 copy.50
  4.2 3.9 %fusion = (f32[8,128]{1,0:T(8,128)S(1)}, f32[1664,128,8]{1,0,2:T(8,128)}) fusion(pred[128,1664]{0,1:T(8,128)(4,1)S(1)} %iota_compare_fusion, bf16[128,8,128]{0,2,1:T(8,128)(2,1)S(1)} %bitcast.103, bf16[1,2,1664,128]{3,2,1,0:T(8,128)(2,1)S(1)} %get-tuple-element.7), kind=kOutput, calls=%fused_computation.6 | convolution fusion | flops 441318400 | bytes 7720960 | tf_op jit(solution)/shard_map/mqgd,mkd->mgqk/dot_general | solution.py:18
  8.1 0.0 copy-done.1
  8.1 0.0 slice-start
  8.1 0.2 copy.51
  8.3 0.0 slice-start.1
  8.3 0.0 copy-start.2
  8.3 7.1 %fusion.2 = (f32[8,128]{1,0:T(8,128)S(1)}, f32[8,128]{1,0:T(8,128)S(1)}, f32[1664,128,8]{1,0,2:T(8,128)}) fusion(f32[1664,128,8]{1,0,2:T(8,128)} %get-tuple-element.14, f32[8,128]{1,0:T(8,128)S(1)} %get-tuple-element.13, pred[128,1664]{0,1:T(8,128)(4,1)S(1)} %iota_compare_fusion, bf16[128,8,128]{0,2,1:T(8,128)(2,1)S(1)} %bitcast.104, ...), kind=kOutput, calls=%fused_computation.8 | convolution fusion | flops 449837056 | bytes 14544896 | tf_op jit(solution)/shard_map/mqgd,mkd->mgqk/dot_general | solution.py:18
  15.4 0.0 slice-done
  15.4 0.0 slice-done.1
  15.4 0.0 copy-done.2
  15.4 2.6 %fusion.17 = bf16[1,128,8,128]{3,1,2,0:T(8,128)(2,1)S(1)} fusion(f32[8,128]{1,0:T(8,128)S(1)} %get-tuple-element.5, f32[8,128]{1,0:T(8,128)S(1)} %get-tuple-element.13, f32[1664,128,8]{1,0,2:T(8,128)S(1)} %bitcast.102, pred[128,1664]{0,1:T(8,128)(4,1)S(1)} %iota_compare_fusion, bf16[1,2,1664,128]{3,2,1,0:T(8,128)(2,1)S(1)} %copy-done.2), kind=kOutput, calls=%fused_computation.17 | convolution fusion | flops 446562304 | bytes 7725056 | tf_op jit(solution)/shard_map/mgqk,mkd->mqgd/dot_general | solution.py:29
  17.9 0.0 copy-start.3
  18.0 0.2 copy.38
  18.1 0.1 concatenate.12
  18.3 0.0 copy-start
  18.3 4.7 %fusion.3 = f32[8,128]{1,0:T(8,128)S(1)} fusion(f32[1664,128,8]{1,0,2:T(8,128)} %get-tuple-element.15, f32[8,128]{1,0:T(8,128)S(1)} %get-tuple-element.6, pred[128,1664]{0,1:T(8,128)(4,1)S(1)} %iota_compare_fusion), kind=kLoop, calls=%fused_computation.9 | loop fusion | flops 8518656 | bytes 7036928 | tf_op jit(solution)/shard_map/reduce_sum | solution.py:27
  23.0 0.0 copy-done.3
  23.0 0.2 copy-done
  23.2 0.0 copy-start.5
  23.2 0.0 copy-start.4
  23.2 2.6 %fusion.14 = bf16[1,128,8,128]{3,1,2,0:T(8,128)(2,1)S(1)} fusion(f32[8,128]{1,0:T(8,128)S(1)} %fusion.3, f32[8,128]{1,0:T(8,128)S(1)} %get-tuple-element.6, f32[1664,128,8]{1,0,2:T(8,128)S(1)} %copy-done, pred[128,1664]{0,1:T(8,128)(4,1)S(1)} %iota_compare_fusion, bf16[1,2,1664,128]{3,2,1,0:T(8,128)(2,1)S(1)} %copy-done.3), kind=kOutput, calls=%fused_computation.16 | convolution fusion | flops 446562304 | bytes 7725056 | tf_op jit(solution)/shard_map/mgqk,mkd->mqgd/dot_general | solution.py:29
  25.8 0.2 copy.42
  26.0 0.1 concatenate.13
  26.1 0.8 pad_maximum_fusion.heads_ref
  27.0 0.0 copy-done.5
  27.0 0.0 copy-done.4
  27.1 0.1 copy.43
  27.1 0.1 copy.44
  27.2 0.7 fusion.24.share_ref
  27.9 116.3 %shard_map.82 = bf16[2,64,2048]{2,1,0:T(8,128)(2,1)} custom-call(bf16[2,16,8,1024]{3,2,1,0:T(8,128)(2,1)} %pad_maximum_fusion.heads_ref, bf16[2,64,2048]{2,1,0:T(8,128)(2,1)} %res_ref.1, f32[1,2048]{1,0:T(1,128)} %bitcast.105, bf16[2,64,128]{2,1,0:T(8,128)(2,1)} %fusion.24.share_ref, bf16[1,2048,1536]{2,1,0:T(8,128)(2,1)} %gu_hbm.1, bf16[1,768,2048]{2,1,0:T(8,128)(2,1)} %dn_hbm.1), custom_call_target="tpu_custom_call" | custom-call | tf_op jit(solution)/shard_map/pallas_call | solution.py:353
  144.2 1.9 %copy.53 = bf16[2,64,2048]{2,1,0:T(8,128)(2,1)} copy(bf16[2,64,2048]{2,1,0:T(8,128)(2,1)} %shard_map.82) | data formatting | bytes 1048576
  (6 shorter events, 0.1 us)
Async XLA Ops:
  2.6 5.5 %copy-start.1 = (bf16[1,2,1664,128]{3,2,1,0:T(8,128)(2,1)}, bf16[1,2,1664,128]{3,2,1,0:T(8,128)(2,1)S(1)}, u32[]{:S(2)}) copy-start(bf16[1,2,1664,128]{3,2,1,0:T(8,128)(2,1)S(1)} %get-tuple-element.7) | copy-start | bytes 2555908
  8.1 7.3 %slice-start = ((s8[6815744]{0:T(1024)(128)(4,1)}), s8[2621440]{0:T(1024)(128)(4,1)S(1)}, s32[]{:S(2)}) async-start(s8[6815744]{0:T(1024)(128)(4,1)} %bitcast.101), calls=%async_computation | async-start | bytes 5242880
  8.3 7.1 %slice-start.1 = ((s8[6815744]{0:T(1024)(128)(4,1)}), s8[4194304]{0:T(1024)(128)(4,1)S(1)}, s32[]{:S(2)}) async-start(s8[6815744]{0:T(1024)(128)(4,1)} %bitcast.101), calls=%async_computation.1 | async-start | bytes 8388608
  8.3 7.1 %copy-start.2 = (bf16[1,2,1664,128]{3,2,1,0:T(8,128)(2,1)S(1)}, bf16[1,2,1664,128]{3,2,1,0:T(8,128)(2,1)}, u32[]{:S(2)}) copy-start(bf16[1,2,1664,128]{3,2,1,0:T(8,128)(2,1)} %copy-done.1) | copy-start | bytes 2555908
  17.9 5.0 %copy-start.3 = (bf16[1,2,1664,128]{3,2,1,0:T(8,128)(2,1)S(1)}, bf16[1,2,1664,128]{3,2,1,0:T(8,128)(2,1)}, u32[]{:S(2)}) copy-start(bf16[1,2,1664,128]{3,2,1,0:T(8,128)(2,1)} %get-tuple-element.8) | copy-start | bytes 2555908
  18.3 4.9 %copy-start = (f32[1664,128,8]{1,0,2:T(8,128)S(1)}, f32[1664,128,8]{1,0,2:T(8,128)}, u32[]{:S(2)}) copy-start(f32[1664,128,8]{1,0,2:T(8,128)} %get-tuple-element.15) | copy-start | bytes 20447236
  23.2 3.8 %copy-start.5 = (s32[2,64,8]{1,2,0:T(8,128)S(1)}, s32[2,64,8]{1,2,0:T(8,128)}, u32[]{:S(2)}) copy-start(s32[2,64,8]{1,2,0:T(8,128)} %param.15) | copy-start | bytes 12292
  23.2 3.8 %copy-start.4 = (s32[2,64,8]{1,2,0:T(8,128)S(1)}, s32[2,64,8]{1,2,0:T(8,128)}, u32[]{:S(2)}) copy-start(s32[2,64,8]{1,2,0:T(8,128)} %param.14) | copy-start | bytes 12292

commit v4 on v3

--- a/solution.py
+++ b/solution.py
@@ -9,27 +9,59 @@
 from jax.sharding import PartitionSpec as P
 
 
-def attend(query_rows, cached_pairs):
-    batches, length, feat_width = query_rows.shape
-    context = cached_pairs.shape[2]
-    head_size = cached_pairs.shape[3]
-    groups = feat_width // head_size
-    head_rows = query_rows.reshape(batches, length, groups, head_size)
-    scores = jnp.einsum(
-        "mqgd,mkd->mgqk", head_rows, cached_pairs[:, 0], preferred_element_type=jnp.float32
-    ) / math.sqrt(head_size)
-    query_pos = context - length + lax.broadcasted_iota(jnp.int32, (length, context), 0)
-    key_pos = lax.broadcasted_iota(jnp.int32, (length, context), 1)
-    allowed = key_pos <= query_pos
-    scores = jnp.where(allowed, scores, -1e30)
-    highest = jnp.max(scores, axis=-1, keepdims=True)
-    scaled_exp = jnp.where(allowed, jnp.exp(scores - highest), 0.0)
-    totals = jnp.sum(scaled_exp, axis=-1, keepdims=True)
-    weights = (scaled_exp / totals).astype(jnp.bfloat16)
-    blended = jnp.einsum(
-        "mgqk,mkd->mqgd", weights, cached_pairs[:, 1], preferred_element_type=jnp.float32
-    )
-    return blended.astype(jnp.bfloat16).reshape(batches, length, feat_width)
+def attend_kernel(heads, q_ref, kv_ref, out_ref):
+    length = q_ref.shape[1]
+    context, head_size = kv_ref.shape[3:]
+    past = context - length
+    keys = kv_ref[0, 0, 0]
+    query = jnp.concatenate(
+        [q_ref[0, :, head * head_size : (head + 1) * head_size] for head in range(heads)], axis=0
+    )
+    scores = lax.dot_general(
+        query, keys, (((1,), (1,)), ((), ())), preferred_element_type=jnp.float32
+    )
+    scores = scores * (1.0 / math.sqrt(head_size))
+    old, new = scores[:, :past], scores[:, past:]
+    row = lax.broadcasted_iota(jnp.int32, new.shape, 0) % length
+    col = lax.broadcasted_iota(jnp.int32, new.shape, 1)
+    allowed = col <= row
+    new = jnp.where(allowed, new, -1e30)
+    highest = jnp.maximum(
+        jnp.max(old, axis=-1, keepdims=True), jnp.max(new, axis=-1, keepdims=True)
+    )
+    old = jnp.exp(old - highest)
+    new = jnp.where(allowed, jnp.exp(new - highest), 0.0)
+    totals = jnp.sum(old, axis=-1, keepdims=True) + jnp.sum(new, axis=-1, keepdims=True)
+    share = 1.0 / totals
+    blended = jnp.dot(
+        (old * share).astype(jnp.bfloat16), kv_ref[0, 0, 1, :past, :],
+        preferred_element_type=jnp.float32,
+    ) + jnp.dot(
+        (new * share).astype(jnp.bfloat16), kv_ref[0, 0, 1, past:, :],
+        preferred_element_type=jnp.float32,
+    )
+    for head in range(heads):
+        out_ref[0, :, head * head_size : (head + 1) * head_size] = blended[
+            head * length : (head + 1) * length
+        ].astype(jnp.bfloat16)
+
+
+def attend_local(queries, keys_values):
+    batches, unit, length, feat_width = queries.shape
+    context, head_size = keys_values.shape[3:]
+    heads = 2
+    wide = heads * head_size
+    return pl.pallas_call(
+        functools.partial(attend_kernel, heads),
+        grid=(batches, feat_width // wide),
+        out_shape=jax.ShapeDtypeStruct((batches, length, feat_width), jnp.bfloat16),
+        in_specs=[
+            pl.BlockSpec((1, length, wide), lambda b, h: (b, 0, h)),
+            pl.BlockSpec((1, 1, 2, context, head_size), lambda b, h: (b, 0, 0, 0, 0)),
+        ],
+        out_specs=pl.BlockSpec((1, length, wide), lambda b, h: (b, 0, h)),
+        compiler_params=pltpu.CompilerParams(vmem_limit_bytes=40 * 1024 * 1024),
+    )(queries.reshape(batches, length, feat_width), keys_values)
 
 
 def to_owners(exchanged, kv_heads):
@@ -386,17 +418,12 @@
     model_width = residual.shape[2]
     kv_heads = model_width // queries.shape[3]
     experts = devices * gate_up.shape[0]
-    own_query = queries[:, 0]
-    own_pairs = keys_values[:, 0]
-    batches, length, feat_width = own_query.shape
+    batches, unit, length, feat_width = queries.shape
     positions = length // devices
     weights = dense_shares(expert_ids, expert_gates, experts)
-    blended = [
-        attend(own_query[index : index + 1], own_pairs[index : index + 1])
-        for index in range(batches)
-    ]
+    blended = attend_local(queries, keys_values)
     if batches == 2 and fits(devices, residual.shape[1], model_width, down_proj.shape[1]):
-        heads = jnp.concatenate(blended).reshape(batches, devices, positions, feat_width)
+        heads = blended.reshape(batches, devices, positions, feat_width)
         lanes = share_lanes(weights)
         return routed_layer(heads, residual, norm_gain, lanes, gate_up, down_proj, kv_heads)
     weights = lax.all_gather(weights, "dev", axis=1, tiled=True)

time: 146 us -> 134 us (0.918)
  matrix products: 16.1 us -> 0 us
  Pallas kernels: 116 us -> 126 us
  other arithmetic: 6.44 us -> 2.21 us
  local copies, waits for them, and re-layouts: 7.06 us -> 5.33 us
    dot_general x4 -> x0, matrix products: 16.1 us -> none  [the longest x2 11 us: attend(): jnp.einsum('mqgd,mkd->mgqk', head_rows, cached_pairs[:, 0], preferred_ele...]
    pallas_call x0 -> x1, Pallas kernels: none -> 9.86 us  [attend_local(): pl.pallas_call(functools.partial(attend_kernel, heads), grid=(batches, fe...]
    reduce_sum x1 -> x0, other arithmetic: 4.69 us -> none  [attend(): totals = jnp.sum(scaled_exp, axis=-1, keepdims=True)]
    slice x2 -> x0, local copies, waits for them, and re-layouts: 3.83 us -> none  [the longest x1 2.46 us: body(): own_pairs[index:index + 1]]
    unnamed x19 -> x7, local copies, waits for them, and re-layouts: 2.47 us -> 5.16 us
where the time goes in v4:
time: 134 us
  Pallas kernels  126 us (94%)
  local copies, waits for them, and re-layouts  5.33 us (4%)
  other arithmetic  2.21 us (2%)
    pallas_call x1, Pallas kernels, routed_layer(): pl.pallas_call(functools.partial(moe_kernel, chips), out_shape=jax.ShapeD...  116 us
    pallas_call x1, Pallas kernels, attend_local(): pl.pallas_call(functools.partial(attend_kernel, heads), grid=(batches, fe...  9.86 us
    unnamed x7, local copies, waits for them, and re-layouts  5.16 us

profile of v4, /device:TPU:0, one launch (start us, length us, event | category | flops | bytes accessed | tf_op | source)
XLA Modules:
  0.0 133.8 jit_solution(17062319779701729870)
XLA Ops:
  0.0 0.8 convert_divide_fusion
  0.8 0.7 select_reduce_fusion
  1.5 0.1 copy.14
  1.6 0.1 copy.13
  1.7 0.7 fusion.2.share_ref
  2.4 0.0 copy-start.1
  2.4 1.5 %copy-done.1 = bf16[2,1,2,1664,128]{4,3,2,1,0:T(8,128)(2,1)S(1)} copy-done((bf16[2,1,2,1664,128]{4,3,2,1,0:T(8,128)(2,1)S(1)}, bf16[2,1,2,1664,128]{4,3,2,1,0:T(8,128)(2,1)}, u32[]{:S(2)}) %copy-start.1) | copy-done | bytes 1703960
  3.9 0.0 copy-start.2
  3.9 1.0 copy-done.2
  4.9 9.9 %shard_map.82 = bf16[2,128,1024]{2,1,0:T(8,128)(2,1)S(1)} custom-call(bf16[2,128,1024]{2,1,0:T(8,128)(2,1)S(1)} %bitcast.4, bf16[2,1,2,1664,128]{4,3,2,1,0:T(8,128)(2,1)S(1)} %copy-done.1), custom_call_target="tpu_custom_call" | custom-call | tf_op jit(solution)/shard_map/pallas_call | solution.py:54
  14.8 0.0 copy-start
  14.8 0.8 copy-done
  15.6 116.3 %shard_map.83 = bf16[2,64,2048]{2,1,0:T(8,128)(2,1)} custom-call(bf16[2,16,8,1024]{3,2,1,0:T(8,128)(2,1)} %bitcast.3, bf16[2,64,2048]{2,1,0:T(8,128)(2,1)} %res_ref.1, f32[1,2048]{1,0:T(1,128)} %bitcast.5, bf16[2,64,128]{2,1,0:T(8,128)(2,1)} %fusion.2.share_ref, bf16[1,2048,1536]{2,1,0:T(8,128)(2,1)} %gu_hbm.1, bf16[1,768,2048]{2,1,0:T(8,128)(2,1)} %dn_hbm.1), custom_call_target="tpu_custom_call" | custom-call | tf_op jit(solution)/shard_map/pallas_call | solution.py:385
  131.9 1.9 %copy.17 = bf16[2,64,2048]{2,1,0:T(8,128)(2,1)} copy(bf16[2,64,2048]{2,1,0:T(8,128)(2,1)} %shard_map.83) | data formatting | bytes 1048576
  (2 shorter events, 0.0 us)
Async XLA Ops:
  2.4 1.5 %copy-start.1 = (bf16[2,1,2,1664,128]{4,3,2,1,0:T(8,128)(2,1)S(1)}, bf16[2,1,2,1664,128]{4,3,2,1,0:T(8,128)(2,1)}, u32[]{:S(2)}) copy-start(bf16[2,1,2,1664,128]{4,3,2,1,0:T(8,128)(2,1)} %kv_ref.1) | copy-start | bytes 5111812
  3.9 1.0 copy-start.2
  14.8 0.8 copy-start

commit v5 on v4

--- a/solution.py
+++ b/solution.py
@@ -9,13 +9,12 @@
 from jax.sharding import PartitionSpec as P
 
 
-def attend_kernel(heads, q_ref, kv_ref, out_ref):
-    length = q_ref.shape[1]
-    context, head_size = kv_ref.shape[3:]
+def attend_pair(heads, pair_rows, keys, values):
+    length = pair_rows.shape[0]
+    context, head_size = keys.shape
     past = context - length
-    keys = kv_ref[0, 0, 0]
     query = jnp.concatenate(
-        [q_ref[0, :, head * head_size : (head + 1) * head_size] for head in range(heads)], axis=0
+        [pair_rows[:, head * head_size : (head + 1) * head_size] for head in range(heads)], axis=0
     )
     scores = lax.dot_general(
         query, keys, (((1,), (1,)), ((), ())), preferred_element_type=jnp.float32
@@ -34,12 +33,19 @@
     totals = jnp.sum(old, axis=-1, keepdims=True) + jnp.sum(new, axis=-1, keepdims=True)
     share = 1.0 / totals
     blended = jnp.dot(
-        (old * share).astype(jnp.bfloat16), kv_ref[0, 0, 1, :past, :],
+        (old * share).astype(jnp.bfloat16), values[:past],
         preferred_element_type=jnp.float32,
     ) + jnp.dot(
-        (new * share).astype(jnp.bfloat16), kv_ref[0, 0, 1, past:, :],
+        (new * share).astype(jnp.bfloat16), values[past:],
         preferred_element_type=jnp.float32,
     )
+    return blended
+
+
+def attend_kernel(heads, q_ref, kv_ref, out_ref):
+    length = q_ref.shape[1]
+    head_size = kv_ref.shape[4]
+    blended = attend_pair(heads, q_ref[0], kv_ref[0, 0, 0], kv_ref[0, 0, 1])
     for head in range(heads):
         out_ref[0, :, head * head_size : (head + 1) * head_size] = blended[
             head * length : (head + 1) * length
@@ -99,8 +105,8 @@
 
 
 def moe_kernel(
-    chips, heads_ref, res_ref, gain_ref, share_ref, gu_hbm, dn_hbm, out_ref,
-    attn, stream, gathered, partial, pairbuf, ringbuf, gu, dn, xs, sh, act,
+    chips, q_ref, kv_ref, res_ref, gain_ref, share_ref, gu_hbm, dn_hbm, out_ref,
+    heads_ref, attn, stream, gathered, partial, pairbuf, ringbuf, gu, dn, xs, sh, act,
     load_sem, ex_send, ex_recv, ag_send, ag_recv, agp_send, agp_recv, rsp_send, rsp_recv, rs_send, rs_recv,
 ):
     batches, rows, width = res_ref.shape
@@ -181,9 +187,23 @@
         target = (me + k) % devices
         pl.semaphore_signal(barrier, inc=1, device_id={"dev": target}, device_id_type=MESH)
 
-    pl.semaphore_wait(barrier, devices - 1)
-
-    for batch in range(batches):
+    head_size = kv_ref.shape[3]
+    for batch in range(batches):
+
+        @pl.loop(0, part // (2 * head_size))
+        def _(h):
+            cols = pl.ds(pl.multiple_of(h * 2 * head_size, 2 * head_size), 2 * head_size)
+            blended = attend_pair(2, q_ref[batch, :, cols], kv_ref[batch, 0], kv_ref[batch, 1])
+            length = q_ref.shape[1]
+            for head in range(2):
+                at = pl.ds(pl.multiple_of((h * 2 + head) * head_size, head_size), head_size)
+                piece = blended[head * length : (head + 1) * length]
+                heads_ref[batch, :, :, at] = piece.reshape(
+                    devices, length // devices, head_size
+                ).astype(jnp.bfloat16)
+
+        if batch == 0:
+            pl.semaphore_wait(barrier, devices - 1)
 
         @pl.loop(1, devices)
         def _(k):
@@ -372,9 +392,10 @@
     return jnp.pad(both, ((0, 0), (0, 0), (0, gap))).astype(jnp.bfloat16)
 
 
-def routed_layer(heads, residual, norm_gain, lanes, gate_up, down_proj, kv_heads):
+def routed_layer(queries, keys_values, residual, norm_gain, lanes, gate_up, down_proj, kv_heads, devices):
     batches, rows, width = residual.shape
-    devices, span, part = heads.shape[1:]
+    length, part = queries.shape[1:]
+    span = length // devices
     hidden = down_proj.shape[1]
     chips = devices // 2
     far = chips // 2
@@ -385,9 +406,10 @@
     return pl.pallas_call(
         functools.partial(moe_kernel, chips),
         out_shape=jax.ShapeDtypeStruct((batches, rows, width), kind),
-        in_specs=[vmem, vmem, vmem, vmem, anywhere, anywhere],
+        in_specs=[vmem, vmem, vmem, vmem, vmem, anywhere, anywhere],
         out_specs=vmem,
         scratch_shapes=[
+            pltpu.VMEM((batches, devices, span, part), kind),
             pltpu.VMEM((batches, devices // kv_heads, kv_heads, span, part), kind),
             pltpu.VMEM((batches, rows, width), jnp.float32),
             pltpu.VMEM((batches, chips, 2, rows, width + 128), kind),
@@ -409,7 +431,7 @@
         compiler_params=pltpu.CompilerParams(
             collective_id=0, has_side_effects=True, vmem_limit_bytes=56 * 1024 * 1024
         ),
-    )(heads, residual, norm_gain.reshape(1, width), lanes, gate_up, down_proj)
+    )(queries, keys_values, residual, norm_gain.reshape(1, width), lanes, gate_up, down_proj)
 
 
 def body(queries, keys_values, residual, norm_gain, gate_up, down_proj, expert_ids, expert_gates):
@@ -421,11 +443,13 @@
     batches, unit, length, feat_width = queries.shape
     positions = length // devices
     weights = dense_shares(expert_ids, expert_gates, experts)
+    if batches == 2 and fits(devices, residual.shape[1], model_width, down_proj.shape[1]):
+        lanes = share_lanes(weights)
+        return routed_layer(
+            queries[:, 0], keys_values[:, 0], residual, norm_gain, lanes, gate_up, down_proj,
+            kv_heads, devices,
+        )
     blended = attend_local(queries, keys_values)
-    if batches == 2 and fits(devices, residual.shape[1], model_width, down_proj.shape[1]):
-        heads = blended.reshape(batches, devices, positions, feat_width)
-        lanes = share_lanes(weights)
-        return routed_layer(heads, residual, norm_gain, lanes, gate_up, down_proj, kv_heads)
     weights = lax.all_gather(weights, "dev", axis=1, tiled=True)
     mine = jnp.sum(
         jnp.where(jnp.arange(experts, dtype=jnp.int32) == me, weights, 0.0), axis=-1, keepdims=True

time: 134 us -> 125 us (0.933)
  Pallas kernels: 126 us -> 120 us
  local copies, waits for them, and re-layouts: 5.33 us -> 2.05 us
    pallas_call x1 -> x0, Pallas kernels: 9.86 us -> none  [attend_local(): pl.pallas_call(functools.partial(attend_kernel, heads), grid=(batches, fe...]
    pallas_call x1, Pallas kernels: 116 us -> 120 us  [routed_layer(): pl.pallas_call(functools.partial(moe_kernel, chips), out_shape=jax.ShapeD...]
    unnamed x7 -> x1, local copies, waits for them, and re-layouts: 5.16 us -> 1.88 us
where the time goes in v5:
time: 125 us; the launch traced here: 124 us
  Pallas kernels  120 us (96%)
  other arithmetic  2.23 us (2%)
  local copies, waits for them, and re-layouts  2.05 us (2%)
    pallas_call x1, Pallas kernels, routed_layer(): pl.pallas_call(functools.partial(moe_kernel, chips), out_shape=jax.ShapeD...  120 us

profile of v5, /device:TPU:0, one launch (start us, length us, event | category | flops | bytes accessed | tf_op | source)
XLA Modules:
  0.0 124.3 jit_solution(8052917215820028321)
XLA Ops:
  0.0 0.8 convert_divide_fusion
  0.8 0.7 select_reduce_fusion
  1.5 0.1 copy.14
  1.6 0.1 copy.13
  1.7 0.7 fusion.2.share_ref
  2.4 119.9 %shard_map.82 = bf16[2,64,2048]{2,1,0:T(8,128)(2,1)} custom-call(bf16[2,128,1024]{2,1,0:T(8,128)(2,1)} %bitcast.4, bf16[2,2,1664,128]{3,2,1,0:T(8,128)(2,1)} %bitcast.3, bf16[2,64,2048]{2,1,0:T(8,128)(2,1)} %res_ref.1, f32[1,2048]{1,0:T(1,128)} %bitcast.5, bf16[2,64,128]{2,1,0:T(8,128)(2,1)} %fusion.2.share_ref, bf16[1,2048,1536]{2,1,0:T(8,128)(2,1)} %gu_hbm.1, ...), custom_call_target="tpu_custom_call" | custom-call | tf_op jit(solution)/shard_map/pallas_call | solution.py:406
  122.4 1.9 %copy.17 = bf16[2,64,2048]{2,1,0:T(8,128)(2,1)} copy(bf16[2,64,2048]{2,1,0:T(8,128)(2,1)} %shard_map.82) | data formatting | bytes 1048576
  (2 shorter events, 0.0 us)
